TPU v7x, 32 devices: a whole 2x2x4 slice. The times are simulated.
32 devices in a mesh: group: 2 (over y), ctx: 4 (over z), smp: 2 (over x), head: 2 (over core).
Axes of the slice: x: 2, y: 2, z: 4, core: 2. Of those that a mesh axis runs over, the one named last changes fastest.
Arguments:
- queries: bfloat16 [512, 2, 4096], P(('group', 'smp'), 'head'), parts along dimension 0, may hold values from -8 to 8
- prefix_cache: bfloat16 [2, 8192, 2, 512], P(None, ('group', 'ctx'), 'head'), parts along dimension 1, may hold values from -8 to 8
- suffix_cache: bfloat16 [2, 512, 128, 2, 512], P(None, ('group', 'ctx', 'smp'), None, 'head'), parts along dimension 1, may hold values from -8 to 8
- suffix_length: int32 [512], P(('group', 'smp')), parts along dimension 0, may hold values from 1 to 128, as said below
- cache_sample: int32 [512], P('group'), parts along dimension 0, may hold values from 0 to 255, as said below
- residual: bfloat16 [512, 8192], P(('group', 'ctx', 'head'), 'smp'), parts along dimension 0, may hold values from -6 to 6
- w_out: bfloat16 [2, 4096, 8192], P('head', 'ctx', 'smp'), may hold values from -0.75 to 0.75
- norm_gain: float32 [8192], P('smp'), may hold values from 0.1 to 1.9
- gate_matrix: bfloat16 [8192, 16384], P('smp', ('ctx', 'head')), may hold values from -0.0625 to 0.0625
- w_up: bfloat16 [8192, 16384], P('smp', ('ctx', 'head')), may hold values from -0.0625 to 0.0625
- w_down: bfloat16 [16384, 8192], P(('ctx', 'head'), 'smp'), may hold values from -0.046875 to 0.046875
Outputs:
- mixed: bfloat16 [512, 8192], P(('group', 'ctx', 'head'), 'smp'), parts along dimension 0
There are 2 independent parts, one for each index of `group`. A program takes and returns all parts, laid end to end along the dimension named above; an argument that names none is the same for every part. Nothing has to cross between parts.
Inputs may be any that keep to these rules, and one draw needn't show every extreme that they name: `suffix_length`: the longest is exactly 128 in every draw. A permutation; cache row r and sample cache_sample[r] lie in the same group, the group of row r being (r // 32) % (2) and that of sample i being i // 128.
All inputs are finite; a program needn't handle non-finite values.
Results may differ from a plain program's by a relative error of at most 0.012.
Values may be sent and summed in bfloat16 or wider, within the bound.
A program may use at most 192 MiB of HBM per device.

v0:
```python
import jax
import jax.numpy as jnp
from jax import lax
from jax.sharding import PartitionSpec as P

D = 8192
QUERY_HEADS = 64
KEY_VALUE_HEADS = 8
HD = 128


EPSILON = 1e-05


def suffix_piece(row_queries, suffix_cache, row_lengths, key_value_heads_here, score_scale):
    rows_here = suffix_cache.shape[1]
    suffix_keys = suffix_cache[0].reshape(rows_here, -1, key_value_heads_here, HD)
    suffix_values = suffix_cache[1].reshape(rows_here, -1, key_value_heads_here, HD)
    row_scores = (
        jnp.einsum("rjgd,rtjd->rjgt", row_queries, suffix_keys, preferred_element_type=jnp.float32)
        * score_scale
    )
    positions = lax.broadcasted_iota(jnp.int32, row_scores.shape, 3)
    row_scores = jnp.where(positions < row_lengths[:, None, None, None], row_scores, -jnp.inf)
    row_high = jnp.max(row_scores, axis=3)
    row_weights = jnp.exp(row_scores - row_high[..., None])
    row_totals = jnp.sum(row_weights, axis=3)
    row_summed = jnp.einsum(
        "rjgt,rtjd->rjgd",
        row_weights.astype(jnp.bfloat16),
        suffix_values,
        preferred_element_type=jnp.float32,
    )
    row_output = (row_summed / row_totals[..., None]).astype(jnp.bfloat16)
    return (row_output, row_high + jnp.log(row_totals))


def merge_pieces(pieces):
    piece_values, piece_lse = pieces
    item_count = piece_values.shape[0]
    peak = jnp.max(piece_lse, axis=1, keepdims=True)
    piece_weights = jnp.exp(piece_lse - peak)
    shaped = piece_values.reshape(item_count, piece_values.shape[1], piece_lse.shape[2], HD)
    numer = jnp.sum(piece_weights[..., None] * shaped, axis=1)
    denom = jnp.sum(piece_weights, axis=1)
    return (numer / denom[..., None]).reshape(item_count, -1).astype(jnp.bfloat16)


def activate(gate_sum, up_sum, square_sum):
    factor = lax.rsqrt(square_sum / D + EPSILON)[:, None]
    return (jax.nn.silu(factor * gate_sum) * (factor * up_sum)).astype(jnp.bfloat16)


def on_device(
    queries,
    prefix_cache,
    suffix_cache,
    suffix_length,
    cache_sample,
    residual,
    w_out,
    norm_gain,
    gate_matrix,
    w_up,
    w_down,
):
    group_rows = queries.shape[0]
    key_value_heads_here = prefix_cache.shape[3] // HD
    queries_per_key_value = QUERY_HEADS // KEY_VALUE_HEADS
    heads_local = key_value_heads_here * queries_per_key_value
    score_scale = HD ** (-0.5)
    queries_split = queries.reshape(group_rows, key_value_heads_here, queries_per_key_value, HD)
    prefix_keys = prefix_cache[0].reshape(-1, key_value_heads_here, HD)
    prefix_values = prefix_cache[1].reshape(-1, key_value_heads_here, HD)
    scores = (
        jnp.einsum("sjgd,pjd->jsgp", queries_split, prefix_keys, preferred_element_type=jnp.float32)
        * score_scale
    )
    highest = jnp.max(scores, axis=3)
    weights = jnp.exp(scores - highest[..., None])
    totals = jnp.sum(weights, axis=3)
    summed = jnp.einsum(
        "jsgp,pjd->sjgd",
        weights.astype(jnp.bfloat16),
        prefix_values,
        preferred_element_type=jnp.float32,
    )
    prefix_out = (summed / jnp.transpose(totals, (1, 0, 2))[..., None]).astype(jnp.bfloat16)
    prefix_lse = jnp.transpose(highest + jnp.log(totals), (1, 0, 2))
    rows_here = suffix_cache.shape[1]
    flat_index = lax.axis_index("ctx") * lax.axis_size("smp") + lax.axis_index("smp")
    row_ids = lax.dynamic_slice_in_dim(cache_sample, flat_index * rows_here, rows_here, 0)
    local_ids = row_ids % group_rows
    row_queries = jnp.take(queries_split, local_ids, axis=0)
    row_lengths = jnp.take(suffix_length, local_ids, axis=0)
    suffix_out, suffix_lse = suffix_piece(
        row_queries, suffix_cache, row_lengths, key_value_heads_here, score_scale
    )
    onehot = (local_ids[None, :] == jnp.arange(group_rows, dtype=jnp.int32)[:, None]).astype(
        jnp.float32
    )
    present = jnp.sum(onehot, axis=1)[:, None]
    placed_out = jnp.dot(
        onehot,
        suffix_out.reshape(rows_here, -1).astype(jnp.float32),
        precision=lax.Precision.HIGHEST,
    )
    placed_lse = jnp.dot(
        onehot, suffix_lse.reshape(rows_here, heads_local), precision=lax.Precision.HIGHEST
    )
    own_lse = prefix_lse.reshape(group_rows, heads_local)
    other_lse = jnp.where(present > 0, placed_lse, own_lse)
    top = jnp.maximum(own_lse, other_lse)
    own_weight = jnp.exp(own_lse - top)
    other_weight = present * jnp.exp(other_lse - top)
    both_weight = own_weight + other_weight
    own_values = prefix_out.reshape(group_rows, heads_local, HD).astype(jnp.float32)
    other_values = placed_out.reshape(group_rows, heads_local, HD)
    local_out = (
        own_weight[..., None] * own_values + other_weight[..., None] * other_values
    ) / both_weight[..., None]
    local_lse = top + jnp.log(both_weight)
    attn_slice = merge_pieces(
        (
            lax.all_to_all(
                local_out.reshape(group_rows, 1, -1), "ctx", split_axis=2, concat_axis=1, tiled=True
            ),
            lax.all_to_all(
                local_lse.reshape(group_rows, 1, -1), "ctx", split_axis=2, concat_axis=1, tiled=True
            ),
        )
    )
    proj_weight = w_out[0]
    all_attn = lax.all_gather(attn_slice, "smp", axis=0, tiled=True)
    own_state = (
        residual.astype(jnp.float32)
        + lax.psum_scatter(
            jnp.dot(all_attn, proj_weight, preferred_element_type=jnp.float32),
            ("ctx", "head"),
            scatter_dimension=0,
            tiled=True,
        )
    ).astype(jnp.bfloat16)
    state = lax.all_gather(own_state, ("ctx", "head"), axis=0, tiled=True)
    state_wide = state.astype(jnp.float32)
    square_part = jnp.sum(state_wide * state_wide, axis=1)
    scaled = (state_wide * norm_gain).astype(jnp.bfloat16)
    gate_portion = jnp.dot(scaled, gate_matrix, preferred_element_type=jnp.float32)
    up_part = jnp.dot(scaled, w_up, preferred_element_type=jnp.float32)
    gate_sum, up_sum, square_sum = (
        lax.psum(gate_portion.astype(jnp.bfloat16), "smp").astype(jnp.float32),
        lax.psum(up_part.astype(jnp.bfloat16), "smp").astype(jnp.float32),
        lax.psum(square_part.astype(jnp.bfloat16), "smp").astype(jnp.float32),
    )
    activated = activate(gate_sum, up_sum, square_sum)
    ffn_rows = lax.psum_scatter(
        jnp.dot(activated, w_down, preferred_element_type=jnp.float32).astype(jnp.bfloat16),
        ("ctx", "head"),
        scatter_dimension=0,
        tiled=True,
    ).astype(jnp.float32)
    return (own_state.astype(jnp.float32) + ffn_rows).astype(jnp.bfloat16)


def solution(mesh):
    in_specs = (
        P(("group", "smp"), "head", None),
        P(None, ("group", "ctx"), "head", None),
        P(None, ("group", "ctx", "smp"), None, "head", None),
        P(("group", "smp")),
        P("group"),
        P(("group", "ctx", "head"), "smp"),
        P("head", "ctx", "smp"),
        P("smp"),
        P("smp", ("ctx", "head")),
        P("smp", ("ctx", "head")),
        P(("ctx", "head"), "smp"),
    )
    out_specs = P(("group", "ctx", "head"), "smp")
    return jax.shard_map(
        on_device, mesh=mesh, in_specs=in_specs, out_specs=out_specs, check_vma=False
    )
```

profile of v0, /device:TPU:0, one launch (start us, length us, event | category | flops | bytes accessed | tf_op | source)
XLA Modules:
  0.0 360.2 jit_solution(7161917489603728494)
XLA Ops:
  10.4 5.9 %fusion.46 = (bf16[1,32,128,1,512]{4,2,3,1,0:T(8,128)(2,1)}, bf16[1,32,128,1,512]{4,2,3,1,0:T(8,128)(2,1)}) fusion(bf16[2,32,128,1,512]{4,2,3,1,0:T(8,128)(2,1)} %param.13), kind=kLoop, calls=%fused_computation.77 | loop fusion | bytes 16777216 | tf_op jit(solution)/shard_map/slice | solution.py:18
  16.4 6.4 %copy.57 = bf16[1,32,128,1,512]{2,4,1,3,0:T(8,128)(2,1)} copy(bf16[1,32,128,1,512]{4,2,3,1,0:T(8,128)(2,1)} %get-tuple-element.18) | data formatting | bytes 8388608
  22.8 8.1 %multiply_reduce_fusion = (f32[4,128,8]{1,2,0:T(8,128)S(1)}, f32[4,128,8,1024]{3,1,2,0:T(8,128)}) fusion(bf16[1024,4,128,1]{0,2,3,1:T(8,128)(2,1)S(1)} %bitcast.92, bf16[128,4,8,128]{3,2,1,0:T(8,128)(2,1)S(1)} %bitcast.89), kind=kOutput, calls=%fused_computation.3 | convolution fusion | flops 1082126336 | bytes 18890752 | tf_op jit(solution)/shard_map/sjgd,pjd->jsgp/dot_general | solution.py:76
  32.2 3.5 fusion.48
  36.4 7.7 %fusion.1 = f32[4,128,8]{1,2,0:T(8,128)S(1)} fusion(f32[4,128,8,1024]{3,1,2,0:T(8,128)} %get-tuple-element.22, f32[4,128,8]{1,2,0:T(8,128)S(1)} %get-tuple-element.21), kind=kLoop, calls=%fused_computation.5 | loop fusion | flops 12578816 | bytes 16809984 | tf_op jit(solution)/shard_map/reduce_sum | solution.py:81
  44.9 6.3 %all-to-all-start = ((f32[128,1,32]{0,1,2:T(1,128)}), f32[128,1,32]{0,1,2:T(1,128)S(1)}, u32[]{:S(2)}, u32[]{:S(2)}) async-start(f32[128,1,32]{0,1,2:T(1,128)} %bitcast.8), calls=%async_computation | async-start | bytes 32768 | tf_op jit(solution)/shard_map/all_to_all | solution.py:128
  51.8 6.4 %copy.58 = bf16[1,32,128,1,512]{2,4,1,3,0:T(8,128)(2,1)} copy(bf16[1,32,128,1,512]{4,2,3,1,0:T(8,128)(2,1)} %get-tuple-element.17) | data formatting | bytes 8388608
  58.2 4.5 %fusion.18 = bf16[32,4,8,128]{3,2,1,0:T(8,128)(2,1)S(1)} fusion(bf16[32,128,4,128]{1,3,2,0:T(8,128)(2,1)} %bitcast.91, f32[32,4,8,128]{3,2,1,0:T(8,128)S(1)} %get-tuple-element.24, f32[32,4,8]{2,1,0:T(4,128)S(1)} %fusion.24, f32[32,4,8]{2,1,0:T(4,128)S(1)} %get-tuple-element.23), kind=kOutput, calls=%fused_computation.28 | convolution fusion | flops 34078720 | bytes 4988928 | tf_op jit(solution)/shard_map/rjgt,rtjd->rjgd/dot_general | solution.py:28
  62.7 7.6 %fusion.12 = bf16[128,4,8,128]{0,3,2,1:T(8,128)(2,1)S(1)} fusion(bf16[1024,4,128,1]{0,2,3,1:T(8,128)(2,1)S(1)} %bitcast.96, f32[4,128,8,1024]{3,1,2,0:T(8,128)} %get-tuple-element.22, f32[4,128,8]{1,2,0:T(8,128)S(1)} %get-tuple-element.21, f32[128,4,8]{0,2,1:T(8,128)S(1)} %bitcast.99), kind=kOutput, calls=%fused_computation.22 | convolution fusion | flops 1087373312 | bytes 18907136 | tf_op jit(solution)/shard_map/jsgp,pjd->sjgd/dot_general | solution.py:82
  70.3 2.0 fusion.11
  72.4 5.1 %all-to-all-start.1 = ((f32[128,1,4096]{0,1,2:T(1,128)}), f32[128,1,4096]{0,1,2:T(1,128)S(1)}, u32[]{:S(2)}, u32[]{:S(2)}) async-start(f32[128,1,4096]{0,1,2:T(1,128)} %bitcast.93), calls=%async_computation.1 | async-start | bytes 4194304 | tf_op jit(solution)/shard_map/all_to_all | solution.py:125
  77.5 47.6 %all-to-all-done.1 = f32[128,1,4096]{0,1,2:T(1,128)S(1)} async-done(((f32[128,1,4096]{0,1,2:T(1,128)}), f32[128,1,4096]{0,1,2:T(1,128)S(1)}, u32[]{:S(2)}, u32[]{:S(2)}) %all-to-all-start.1) | async-done | bytes 2097184 | tf_op jit(solution)/shard_map/all_to_all | solution.py:125
  125.4 8.2 %all_gather.6 = bf16[256,1024]{0,1:T(8,128)(2,1)S(1)} all-gather(bf16[128,1024]{0,1:T(8,128)(2,1)S(1)} %bitcast.94), channel_id=1, replica_groups=mesh['group'=2,'ctx'=4,'smp'=2,'head'=2] {'smp'}, dimensions={0}, use_global_device_ids=true | all-gather | bytes 786432 | tf_op jit(solution)/shard_map/all_gather | solution.py:134
  133.6 7.7 %fusion.4 = f32[256,4096]{1,0:T(8,128)} fusion(bf16[256,1024]{0,1:T(8,128)(2,1)S(1)} %all_gather.6, bf16[1,1024,4096]{2,1,0:T(8,128)(2,1)} %param.17), kind=kOutput, calls=%fused_computation.7 | convolution fusion | flops 2147483648 | bytes 13107200 | tf_op jit(solution)/shard_map/dot_general | solution.py:138
  141.4 48.2 %reduce-scatter.3.cloned.1.call-done = f32[32,4096]{1,0:T(8,128)} async-done(((f32[256,4096]{1,0:T(8,128)}), f32[32,4096]{1,0:T(8,128)}) %reduce-scatter.3.cloned.1.call-update) | async-done | bytes 524304 | tf_op jit(solution)/shard_map/reduce_scatter | solution.py:137
  189.6 1.8 add_convert_fusion.1
  191.5 27.7 %all-gather.2.cloned.1.call-done = bf16[256,4096]{1,0:T(8,128)(2,1)} async-done(((bf16[32,4096]{1,0:T(8,128)(2,1)}), bf16[256,4096]{1,0:T(8,128)(2,1)}) %all-gather.2.cloned.1.call-update) | async-done | bytes 2097168 | tf_op jit(solution)/shard_map/all_gather | solution.py:144
  219.2 12.0 %convolution_convert_fusion.1 = bf16[256,2048]{1,0:T(8,128)(2,1)} fusion(bf16[4096,2048]{1,0:T(8,128)(2,1)} %param.20, bf16[256,4096]{1,0:T(8,128)(2,1)} %all-gather.2.cloned.1.call-done, f32[4096]{0:T(1024)S(1)} %copy-done.6), kind=kOutput, calls=%fused_computation.16 | convolution fusion | flops 4298637312 | bytes 19939328 | tf_op jit(solution)/shard_map/dot_general | solution.py:149
  231.2 9.3 %convolution_convert_fusion.2 = bf16[256,2048]{1,0:T(8,128)(2,1)} fusion(bf16[4096,2048]{1,0:T(8,128)(2,1)} %param.19, bf16[256,4096]{1,0:T(8,128)(2,1)S(1)} %copy-done.3, f32[4096]{0:T(1024)S(1)} %copy-done.6), kind=kOutput, calls=%fused_computation.17 | convolution fusion | flops 4298637312 | bytes 19939328 | tf_op jit(solution)/shard_map/dot_general | solution.py:148
  241.1 5.2 %psum.21 = bf16[256]{0:T(256)(128)(2,1)S(1)} all-reduce(bf16[256]{0:T(256)(128)(2,1)S(1)} %fusion.8), channel_id=1, replica_groups=mesh['group'=2,'ctx'=4,'smp'=2,'head'=2] {'smp'}, use_global_device_ids=true, to_apply=%region_10.11 | all-reduce | flops 256 | bytes 1024 | tf_op jit(solution)/shard_map/psum | solution.py:153
  246.2 56.8 %all-reduce.3.cloned.1.call-done = (bf16[256,2048]{1,0:T(8,128)(2,1)}, bf16[256,2048]{1,0:T(8,128)(2,1)}) async-done(((bf16[256,2048]{1,0:T(8,128)(2,1)}, bf16[256,2048]{1,0:T(8,128)(2,1)}), (bf16[256,2048]{1,0:T(8,128)(2,1)}, bf16[256,2048]{1,0:T(8,128)(2,1)})) %all-reduce.3.cloned.1.call-update) | async-done | bytes 2097168 | tf_op jit(solution)/shard_map/psum | solution.py:152
  303.0 12.6 %convolution_convert_fusion = bf16[256,4096]{1,0:T(8,128)(2,1)} fusion(bf16[2048,4096]{1,0:T(8,128)(2,1)} %param.21, bf16[256,2048]{1,0:T(8,128)(2,1)} %get-tuple-element.5, bf16[256,2048]{1,0:T(8,128)(2,1)} %get-tuple-element.6, f32[256]{0:T(256)S(1)} %add_rsqrt_fusion), kind=kOutput, calls=%fused_computation.13 | convolution fusion | flops 4301258752 | bytes 20972544 | tf_op jit(solution)/shard_map/dot_general | solution.py:157
  315.7 36.2 %reduce-scatter.5.cloned.1.call-done = bf16[32,4096]{1,0:T(8,128)(2,1)} async-done(((bf16[256,4096]{1,0:T(8,128)(2,1)}), bf16[32,4096]{1,0:T(8,128)(2,1)}) %reduce-scatter.5.cloned.1.call-update) | async-done | bytes 262160 | tf_op jit(solution)/shard_map/reduce_scatter | solution.py:156
  351.9 1.7 add_convert_fusion
  (44 shorter events, 8.2 us)
Async XLA Ops:
  6.5 25.0 %copy-start = (s32[128]{0:T(128)S(1)}, s32[128]{0:T(128)}, u32[]{:S(2)}) copy-start(s32[128]{0:T(128)} %param.14) | copy-start | bytes 1540
  6.5 3.7 %copy-start.5 = (s32[256]{0:T(256)S(1)}, s32[256]{0:T(256)}, u32[]{:S(2)}) copy-start(s32[256]{0:T(256)} %param.15) | copy-start | bytes 3076
  44.9 27.5 %all-to-all-start = ((f32[128,1,32]{0,1,2:T(1,128)}), f32[128,1,32]{0,1,2:T(1,128)S(1)}, u32[]{:S(2)}, u32[]{:S(2)}) async-start(f32[128,1,32]{0,1,2:T(1,128)} %bitcast.8), calls=%async_computation | async-start | bytes 32768 | tf_op jit(solution)/shard_map/all_to_all | solution.py:128
  72.4 52.7 %all-to-all-start.1 = ((f32[128,1,4096]{0,1,2:T(1,128)}), f32[128,1,4096]{0,1,2:T(1,128)S(1)}, u32[]{:S(2)}, u32[]{:S(2)}) async-start(f32[128,1,4096]{0,1,2:T(1,128)} %bitcast.93), calls=%async_computation.1 | async-start | bytes 4194304 | tf_op jit(solution)/shard_map/all_to_all | solution.py:125
  77.5 112.2 %reduce-scatter.3.cloned.1.call-start = ((), (), s32[]{:S(2)}) async-start(), calls=%async_computation.4 | async-start | bytes 4718592 | tf_op jit(solution)/shard_map/reduce_scatter | solution.py:137
  141.3 48.3 %copy-start.4 = (bf16[32,4096]{1,0:T(8,128)(2,1)S(1)}, bf16[32,4096]{1,0:T(8,128)(2,1)}, u32[]{:S(2)}) copy-start(bf16[32,4096]{1,0:T(8,128)(2,1)} %param.16) | copy-start | bytes 786436
  141.3 77.9 %copy-start.6 = (f32[4096]{0:T(1024)S(1)}, f32[4096]{0:T(1024)}, u32[]{:S(2)}) copy-start(f32[4096]{0:T(1024)} %param.18) | copy-start | bytes 49156
  141.3 77.9 %all-gather.2.cloned.1.call-start = ((), (), s32[]{:S(2)}) async-start(), calls=%async_computation.5 | async-start | bytes 2359296 | tf_op jit(solution)/shard_map/all_gather | solution.py:144
  191.4 111.6 %all-reduce.3.cloned.1.call-start = ((), (), s32[]{:S(2)}) async-start(), calls=%async_computation.7 | async-start | bytes 4194304 | tf_op jit(solution)/shard_map/psum | solution.py:152
  219.2 12.0 %copy-start.3 = (bf16[256,4096]{1,0:T(8,128)(2,1)S(1)}, bf16[256,4096]{1,0:T(8,128)(2,1)}, u32[]{:S(2)}) copy-start(bf16[256,4096]{1,0:T(8,128)(2,1)} %all-gather.2.cloned.1.call-done) | copy-start | bytes 6291460
  240.5 111.4 %reduce-scatter.5.cloned.1.call-start = ((), (), s32[]{:S(2)}) async-start(), calls=%async_computation.6 | async-start | bytes 2359296 | tf_op jit(solution)/shard_map/reduce_scatter | solution.py:156
  303.0 48.9 %copy-start.2 = (bf16[32,4096]{1,0:T(8,128)(2,1)S(1)}, bf16[32,4096]{1,0:T(8,128)(2,1)}, u32[]{:S(2)}) copy-start(bf16[32,4096]{1,0:T(8,128)(2,1)} %add_convert_fusion.1) | copy-start | bytes 786436
  303.0 50.6 %copy-start.1 = (s32[128]{0:T(128)S(1)}, s32[128]{0:T(128)}, u32[]{:S(2)}) copy-start(s32[128]{0:T(128)} %param.14) | copy-start | bytes 1540
Sparse Core Ops, SparseCore 0:
  141.4 48.1 reduce-scatter.2
  191.6 27.6 all-gather.1
  240.6 62.3 all-reduce.2
  315.8 36.0 reduce-scatter.4
where the time goes:
time: 361 us; the launch traced here: 360 us
  waiting for transfers between devices  217 us (60%)
  matrix products  68.3 us (19%)
  local copies, waits for them, and re-layouts  24.4 us (7%)
  blocking collectives  13.4 us (4%)
  between operations  13.2 us (4%)
  other arithmetic  12.6 us (3%)
  starting transfers between devices  11.6 us (3%)
    psum x1, waiting for transfers between devices, on_device(): lax.psum(up_part.astype(jnp.bfloat16), 'smp').astype(jnp.float32)  56.8 us
    reduce_scatter x1, waiting for transfers between devices, on_device(): lax.psum_scatter(jnp.dot(all_attn, proj_weight, preferred_element_type=jn...  48.2 us
    all_to_all x1, waiting for transfers between devices, on_device(): lax.all_to_all(local_out.reshape(group_rows, 1, -1), 'ctx', split_axis=2,...  47.6 us
    reduce_scatter x1, waiting for transfers between devices, on_device(): lax.psum_scatter(jnp.dot(activated, w_down, preferred_element_type=jnp.fl...  36.2 us
    all_gather x1, waiting for transfers between devices, on_device(): state = lax.all_gather(own_state, ('ctx', 'head'), axis=0, tiled=True)  27.7 us
    unnamed x18, local copies, waits for them, and re-layouts  14.8 us
    dot_general x1, matrix products, on_device(): jnp.dot(activated, w_down, preferred_element_type=jnp.float32)  12.6 us
    dot_general x1, matrix products, on_device(): up_part = jnp.dot(scaled, w_up, preferred_element_type=jnp.float32)  12 us
  transfers between devices with their start and end apart: 6, of which 5 were waited for; matrix products, arithmetic and copies ran while one was open for 6% of the time, Pallas kernels for 0%

commit v1 on v0

--- a/solution.py
+++ b/solution.py
@@ -1,6 +1,10 @@
+import functools
+
 import jax
 import jax.numpy as jnp
 from jax import lax
+from jax.experimental import pallas as pl
+from jax.experimental.pallas import tpu as pltpu
 from jax.sharding import PartitionSpec as P
 
 D = 8192
@@ -35,20 +39,487 @@
     return (row_output, row_high + jnp.log(row_totals))
 
 
-def merge_pieces(pieces):
-    piece_values, piece_lse = pieces
-    item_count = piece_values.shape[0]
-    peak = jnp.max(piece_lse, axis=1, keepdims=True)
-    piece_weights = jnp.exp(piece_lse - peak)
-    shaped = piece_values.reshape(item_count, piece_values.shape[1], piece_lse.shape[2], HD)
-    numer = jnp.sum(piece_weights[..., None] * shaped, axis=1)
-    denom = jnp.sum(piece_weights, axis=1)
-    return (numer / denom[..., None]).reshape(item_count, -1).astype(jnp.bfloat16)
-
-
-def activate(gate_sum, up_sum, square_sum):
-    factor = lax.rsqrt(square_sum / D + EPSILON)[:, None]
-    return (jax.nn.silu(factor * gate_sum) * (factor * up_sum)).astype(jnp.bfloat16)
+MESH = pl.DeviceIdType.MESH
+TILE = 512
+VMEM_BYTES = 62 * 1024 * 1024
+
+
+def remote(src, dst, send_sem, recv_sem, where):
+    return pltpu.make_async_remote_copy(
+        src_ref=src,
+        dst_ref=dst,
+        send_sem=send_sem,
+        recv_sem=recv_sem,
+        device_id=where,
+        device_id_type=MESH,
+    )
+
+
+def greet(n, n_smp, c, s, h):
+    barrier = pltpu.get_barrier_semaphore()
+    for k in range(1, n):
+        pl.semaphore_signal(barrier, inc=1, device_id={"ctx": lax.rem(c + k, n)}, device_id_type=MESH)
+    for k in range(1, n_smp):
+        pl.semaphore_signal(
+            barrier, inc=1, device_id={"smp": lax.rem(s + k, n_smp)}, device_id_type=MESH
+        )
+    pl.semaphore_signal(barrier, inc=1, device_id={"head": 1 - h}, device_id_type=MESH)
+    pl.semaphore_wait(barrier, (n - 1) + (n_smp - 1) + 1)
+
+
+class Scatter:
+    def __init__(self, n, c, h, buf_a, recv_a, buf_b, recv_b, sa, ra, sb, rb):
+        self.n, self.c, self.h = n, c, h
+        self.buf_a, self.recv_a, self.buf_b, self.recv_b = buf_a, recv_a, buf_b, recv_b
+        self.sa, self.ra, self.sb, self.rb = sa, ra, sb, rb
+
+    def pair_copy(self, t):
+        return remote(
+            self.buf_a.at[t, 1 - self.h],
+            self.recv_a.at[t],
+            self.sa.at[t],
+            self.ra.at[t],
+            {"head": 1 - self.h},
+        )
+
+    def row_copy(self, t, k):
+        d = lax.rem(self.c + k, self.n)
+        return remote(
+            self.buf_b.at[t, d],
+            self.recv_b.at[t, k - 1],
+            self.sb.at[t, k - 1],
+            self.rb.at[t, k - 1],
+            {"ctx": d},
+        )
+
+    def give(self, t, value):
+        _, _, n, rows, width = self.buf_a.shape
+        parts = value.reshape(n, 2, rows, width).astype(jnp.bfloat16)
+        self.buf_a[t, 0] = parts[:, 0]
+        self.buf_a[t, 1] = parts[:, 1]
+        self.pair_copy(t).start()
+
+    def middle(self, t):
+        self.pair_copy(t).wait()
+        both = self.buf_a[t, self.h].astype(jnp.float32) + self.recv_a[t].astype(jnp.float32)
+        self.buf_b[t] = both.astype(jnp.bfloat16)
+        for k in range(1, self.n):
+            self.row_copy(t, k).start()
+
+    def finish(self, t):
+        total = self.buf_b[t, self.c].astype(jnp.float32)
+        for k in range(1, self.n):
+            self.row_copy(t, k).wait()
+            total = total + self.recv_b[t, k - 1].astype(jnp.float32)
+        return total
+
+
+def columns(t, width):
+    return pl.ds(pl.multiple_of(t * width, width), width)
+
+
+def proj_kernel(
+    n,
+    n_smp,
+    out_ref,
+    lse_ref,
+    w_ref,
+    res_ref,
+    state_ref,
+    out_in,
+    lse_in,
+    attn,
+    w_buf,
+    buf_a,
+    recv_a,
+    buf_b,
+    recv_b,
+    w_sem,
+    os,
+    orr,
+    ls,
+    lr,
+    xs,
+    xr,
+    sa,
+    ra,
+    sb,
+    rb,
+    gs,
+    gr,
+    fs,
+    fr,
+):
+    c, s, h = lax.axis_index("ctx"), lax.axis_index("smp"), lax.axis_index("head")
+    tiles = w_buf.shape[0]
+
+    def w_copy(t):
+        return pltpu.make_async_copy(w_ref.at[:, columns(t, TILE)], w_buf.at[t], w_sem.at[t])
+
+    @pl.loop(0, tiles)
+    def _(t):
+        w_copy(t).start()
+
+    greet(n, n_smp, c, s, h)
+
+    def piece_copies(k):
+        d = lax.rem(c + k, n)
+        return (
+            remote(out_ref.at[d], out_in.at[k - 1], os.at[k - 1], orr.at[k - 1], {"ctx": d}),
+            remote(lse_ref.at[d], lse_in.at[k - 1], ls.at[k - 1], lr.at[k - 1], {"ctx": d}),
+        )
+
+    for k in range(1, n):
+        for copy in piece_copies(k):
+            copy.start()
+    for k in range(1, n):
+        for copy in piece_copies(k):
+            copy.wait()
+
+    lses = [lse_ref[c]] + [lse_in[k] for k in range(n - 1)]
+    peak = functools.reduce(jnp.maximum, lses)
+    scales = [jnp.exp(value - peak) for value in lses]
+    denom = functools.reduce(jnp.add, scales)
+    scales = [value / denom for value in scales]
+    for j in range(lse_ref.shape[2]):
+        lanes = slice(j * HD, (j + 1) * HD)
+        total = scales[0][:, j : j + 1] * out_ref[c, :, lanes].astype(jnp.float32)
+        for k in range(n - 1):
+            total = total + scales[k + 1][:, j : j + 1] * out_in[k, :, lanes].astype(jnp.float32)
+        attn[s, :, lanes] = total.astype(jnp.bfloat16)
+
+    def attn_copy(k):
+        return remote(
+            attn.at[s], attn.at[s], xs.at[k - 1], xr.at[k - 1], {"smp": lax.rem(s + k, n_smp)}
+        )
+
+    for k in range(1, n_smp):
+        attn_copy(k).start()
+    for k in range(1, n_smp):
+        attn_copy(k).wait()
+
+    scatter = Scatter(n, c, h, buf_a, recv_a, buf_b, recv_b, sa, ra, sb, rb)
+
+    @pl.loop(0, tiles)
+    def _(t):
+        w_copy(t).wait()
+        rows = attn[...].reshape(-1, attn.shape[2])
+        scatter.give(t, jnp.dot(rows, w_buf[t], preferred_element_type=jnp.float32))
+
+        @pl.when(t >= 1)
+        def _():
+            scatter.middle(t - 1)
+
+    scatter.middle(tiles - 1)
+
+    def gather_copy(t, k):
+        block = state_ref.at[c, h, :, columns(t, TILE)]
+        return remote(
+            block, block, gs.at[t, k - 1], gr.at[t, k - 1], {"ctx": lax.rem(c + k, n)}
+        )
+
+    def pass_copy(t, k):
+        block = state_ref.at[lax.rem(c + n - k, n), h, :, columns(t, TILE)]
+        return remote(block, block, fs.at[t, k], fr.at[t, k], {"head": 1 - h})
+
+    @pl.loop(0, tiles)
+    def _(t):
+        own = scatter.finish(t) + res_ref[:, columns(t, TILE)].astype(jnp.float32)
+        state_ref[c, h, :, columns(t, TILE)] = own.astype(jnp.bfloat16)
+        for k in range(1, n):
+            gather_copy(t, k).start()
+        pass_copy(t, 0).start()
+
+    @pl.loop(0, tiles)
+    def _(t):
+        for k in range(1, n):
+            gather_copy(t, k).wait()
+            pass_copy(t, k).start()
+
+    @pl.loop(0, tiles)
+    def _(t):
+        for k in range(n):
+            pass_copy(t, k).wait()
+
+
+def project(n, n_smp, out, lse, w, residual):
+    count, group_rows, features = out.shape
+    rows, width = residual.shape
+    tiles = width // TILE
+    vmem = pl.BlockSpec(memory_space=pltpu.VMEM)
+    dma = pltpu.SemaphoreType.DMA
+    bf16 = jnp.bfloat16
+    return pl.pallas_call(
+        functools.partial(proj_kernel, n, n_smp),
+        out_shape=jax.ShapeDtypeStruct((n, 2, rows, width), bf16),
+        in_specs=[vmem, vmem, pl.BlockSpec(memory_space=pl.ANY), vmem],
+        out_specs=vmem,
+        scratch_shapes=[
+            pltpu.VMEM((n - 1, group_rows, features), bf16),
+            pltpu.VMEM((n - 1,) + lse.shape[1:], jnp.float32),
+            pltpu.VMEM((n_smp, group_rows, features), bf16),
+            pltpu.VMEM((tiles, w.shape[0], TILE), bf16),
+            pltpu.VMEM((tiles, 2, n, rows, TILE), bf16),
+            pltpu.VMEM((tiles, n, rows, TILE), bf16),
+            pltpu.VMEM((tiles, n, rows, TILE), bf16),
+            pltpu.VMEM((tiles, n - 1, rows, TILE), bf16),
+            dma((tiles,)),
+            dma((n - 1,)),
+            dma((n - 1,)),
+            dma((n - 1,)),
+            dma((n - 1,)),
+            dma((n_smp - 1,)),
+            dma((n_smp - 1,)),
+            dma((tiles,)),
+            dma((tiles,)),
+            dma((tiles, n - 1)),
+            dma((tiles, n - 1)),
+            dma((tiles, n - 1)),
+            dma((tiles, n - 1)),
+            dma((tiles, n)),
+            dma((tiles, n)),
+        ],
+        compiler_params=pltpu.CompilerParams(
+            collective_id=0, has_side_effects=True, vmem_limit_bytes=VMEM_BYTES
+        ),
+    )(out, lse, w, residual)
+
+
+UNITS = 256
+SLOTS = 4
+
+
+def ffn_kernel(
+    n,
+    n_smp,
+    state_ref,
+    gain_ref,
+    gate_ref,
+    up_ref,
+    down_ref,
+    mixed_ref,
+    scaled,
+    squares,
+    squares_in,
+    gate_buf,
+    up_buf,
+    down_buf,
+    part,
+    part_in,
+    hidden,
+    buf_a,
+    recv_a,
+    buf_b,
+    recv_b,
+    g_sem,
+    u_sem,
+    d_sem,
+    qs,
+    qr,
+    ps,
+    pr,
+    hs,
+    hr,
+    sa,
+    ra,
+    sb,
+    rb,
+):
+    c, s, h = lax.axis_index("ctx"), lax.axis_index("smp"), lax.axis_index("head")
+    steps = part.shape[0]
+    slots = gate_buf.shape[0]
+    tiles = down_buf.shape[0]
+    width = state_ref.shape[3]
+    all_rows = state_ref.shape[0] * 2 * state_ref.shape[2]
+    smp_rows = all_rows // n_smp
+
+    def weight_copies(t):
+        slot = lax.rem(t, slots)
+        return (
+            pltpu.make_async_copy(
+                gate_ref.at[:, columns(t, UNITS)], gate_buf.at[slot], g_sem.at[slot]
+            ),
+            pltpu.make_async_copy(up_ref.at[:, columns(t, UNITS)], up_buf.at[slot], u_sem.at[slot]),
+        )
+
+    def down_copy(t):
+        return pltpu.make_async_copy(down_ref.at[:, columns(t, TILE)], down_buf.at[t], d_sem.at[t])
+
+    @pl.loop(0, min(slots, steps))
+    def _(t):
+        for copy in weight_copies(t):
+            copy.start()
+
+    greet(n, n_smp, c, s, h)
+
+    for block in range(n):
+        wide = state_ref[block].reshape(-1, width).astype(jnp.float32)
+        rows = slice(block * wide.shape[0], (block + 1) * wide.shape[0])
+        scaled[rows] = (wide * gain_ref[...]).astype(jnp.bfloat16)
+        sums = jnp.sum(wide * wide, axis=1, keepdims=True)
+        squares[rows] = jnp.broadcast_to(sums, (wide.shape[0], 128))
+
+    def smp_rows_of(p):
+        return pl.ds(pl.multiple_of(p * smp_rows, smp_rows), smp_rows)
+
+    def square_copy(k):
+        p = lax.rem(s + k, n_smp)
+        return remote(
+            squares.at[smp_rows_of(p)], squares_in.at[k - 1], qs.at[k - 1], qr.at[k - 1], {"smp": p}
+        )
+
+    for k in range(1, n_smp):
+        square_copy(k).start()
+
+    def part_copy(t, k):
+        p = lax.rem(s + k, n_smp)
+        return remote(
+            part.at[t, smp_rows_of(p)],
+            part_in.at[t, k - 1],
+            ps.at[t, k - 1],
+            pr.at[t, k - 1],
+            {"smp": p},
+        )
+
+    def hidden_copy(t, k):
+        block = hidden.at[smp_rows_of(s), columns(t, UNITS)]
+        return remote(
+            block, block, hs.at[t, k - 1], hr.at[t, k - 1], {"smp": lax.rem(s + k, n_smp)}
+        )
+
+    def act(t):
+        both = part[t, smp_rows_of(s)].astype(jnp.float32)
+        for k in range(1, n_smp):
+            part_copy(t, k).wait()
+            both = both + part_in[t, k - 1].astype(jnp.float32)
+        total = squares[smp_rows_of(s)]
+        for k in range(1, n_smp):
+            total = total + squares_in[k - 1]
+        factor = lax.rsqrt(total / (width * n_smp) + EPSILON)[:, :1]
+        gate = factor * both[:, :UNITS]
+        up = factor * both[:, UNITS:]
+        value = gate / (1.0 + jnp.exp(-gate)) * up
+        hidden[smp_rows_of(s), columns(t, UNITS)] = value.astype(jnp.bfloat16)
+        for k in range(1, n_smp):
+            hidden_copy(t, k).start()
+
+    lag = min(2, steps)
+
+    @pl.loop(0, steps)
+    def _(t):
+        for copy in weight_copies(t):
+            copy.wait()
+        slot = lax.rem(t, slots)
+        part[t, :, :UNITS] = jnp.dot(
+            scaled[...], gate_buf[slot], preferred_element_type=jnp.float32
+        ).astype(jnp.bfloat16)
+        part[t, :, UNITS:] = jnp.dot(
+            scaled[...], up_buf[slot], preferred_element_type=jnp.float32
+        ).astype(jnp.bfloat16)
+        for k in range(1, n_smp):
+            part_copy(t, k).start()
+
+        @pl.when(t + slots < steps)
+        def _():
+            for copy in weight_copies(t + slots):
+                copy.start()
+
+        @pl.when(t < tiles)
+        def _():
+            down_copy(t).start()
+
+        @pl.when(t == lag)
+        def _():
+            for k in range(1, n_smp):
+                square_copy(k).wait()
+
+        @pl.when(t >= lag)
+        def _():
+            act(t - lag)
+
+    if steps <= lag:
+        for k in range(1, n_smp):
+            square_copy(k).wait()
+
+    for t in range(steps, tiles):
+        down_copy(t).start()
+
+    @pl.loop(steps - lag, steps)
+    def _(t):
+        act(t)
+
+    @pl.loop(0, steps)
+    def _(t):
+        for k in range(1, n_smp):
+            hidden_copy(t, k).wait()
+
+    scatter = Scatter(n, c, h, buf_a, recv_a, buf_b, recv_b, sa, ra, sb, rb)
+
+    @pl.loop(0, tiles)
+    def _(t):
+        down_copy(t).wait()
+        scatter.give(t, jnp.dot(hidden[...], down_buf[t], preferred_element_type=jnp.float32))
+
+        @pl.when(t >= 1)
+        def _():
+            scatter.middle(t - 1)
+
+    scatter.middle(tiles - 1)
+
+    @pl.loop(0, tiles)
+    def _(t):
+        own = scatter.finish(t) + state_ref[c, h, :, columns(t, TILE)].astype(jnp.float32)
+        mixed_ref[:, columns(t, TILE)] = own.astype(jnp.bfloat16)
+
+
+def feed_forward(n, n_smp, state, gain, gate, up, down):
+    _, _, rows, width = state.shape
+    all_rows = n * 2 * rows
+    smp_rows = all_rows // n_smp
+    units = gate.shape[1]
+    steps, tiles = units // UNITS, width // TILE
+    slots = min(SLOTS, steps)
+    vmem = pl.BlockSpec(memory_space=pltpu.VMEM)
+    hbm = pl.BlockSpec(memory_space=pl.ANY)
+    dma = pltpu.SemaphoreType.DMA
+    bf16 = jnp.bfloat16
+    return pl.pallas_call(
+        functools.partial(ffn_kernel, n, n_smp),
+        out_shape=jax.ShapeDtypeStruct((rows, width), bf16),
+        in_specs=[vmem, vmem, hbm, hbm, hbm],
+        out_specs=vmem,
+        scratch_shapes=[
+            pltpu.VMEM((all_rows, width), bf16),
+            pltpu.VMEM((all_rows, 128), jnp.float32),
+            pltpu.VMEM((n_smp - 1, smp_rows, 128), jnp.float32),
+            pltpu.VMEM((slots, width, UNITS), bf16),
+            pltpu.VMEM((slots, width, UNITS), bf16),
+            pltpu.VMEM((tiles, units, TILE), bf16),
+            pltpu.VMEM((steps, all_rows, 2 * UNITS), bf16),
+            pltpu.VMEM((steps, n_smp - 1, smp_rows, 2 * UNITS), bf16),
+            pltpu.VMEM((all_rows, units), bf16),
+            pltpu.VMEM((tiles, 2, n, rows, TILE), bf16),
+            pltpu.VMEM((tiles, n, rows, TILE), bf16),
+            pltpu.VMEM((tiles, n, rows, TILE), bf16),
+            pltpu.VMEM((tiles, n - 1, rows, TILE), bf16),
+            dma((slots,)),
+            dma((slots,)),
+            dma((tiles,)),
+            dma((n_smp - 1,)),
+            dma((n_smp - 1,)),
+            dma((steps, n_smp - 1)),
+            dma((steps, n_smp - 1)),
+            dma((steps, n_smp - 1)),
+            dma((steps, n_smp - 1)),
+            dma((tiles,)),
+            dma((tiles,)),
+            dma((tiles, n - 1)),
+            dma((tiles, n - 1)),
+        ],
+        compiler_params=pltpu.CompilerParams(
+            collective_id=1, has_side_effects=True, vmem_limit_bytes=VMEM_BYTES
+        ),
+    )(state, gain, gate, up, down)
 
 
 def on_device(
@@ -120,46 +591,11 @@
         own_weight[..., None] * own_values + other_weight[..., None] * other_values
     ) / both_weight[..., None]
     local_lse = top + jnp.log(both_weight)
-    attn_slice = merge_pieces(
-        (
-            lax.all_to_all(
-                local_out.reshape(group_rows, 1, -1), "ctx", split_axis=2, concat_axis=1, tiled=True
-            ),
-            lax.all_to_all(
-                local_lse.reshape(group_rows, 1, -1), "ctx", split_axis=2, concat_axis=1, tiled=True
-            ),
-        )
-    )
-    proj_weight = w_out[0]
-    all_attn = lax.all_gather(attn_slice, "smp", axis=0, tiled=True)
-    own_state = (
-        residual.astype(jnp.float32)
-        + lax.psum_scatter(
-            jnp.dot(all_attn, proj_weight, preferred_element_type=jnp.float32),
-            ("ctx", "head"),
-            scatter_dimension=0,
-            tiled=True,
-        )
-    ).astype(jnp.bfloat16)
-    state = lax.all_gather(own_state, ("ctx", "head"), axis=0, tiled=True)
-    state_wide = state.astype(jnp.float32)
-    square_part = jnp.sum(state_wide * state_wide, axis=1)
-    scaled = (state_wide * norm_gain).astype(jnp.bfloat16)
-    gate_portion = jnp.dot(scaled, gate_matrix, preferred_element_type=jnp.float32)
-    up_part = jnp.dot(scaled, w_up, preferred_element_type=jnp.float32)
-    gate_sum, up_sum, square_sum = (
-        lax.psum(gate_portion.astype(jnp.bfloat16), "smp").astype(jnp.float32),
-        lax.psum(up_part.astype(jnp.bfloat16), "smp").astype(jnp.float32),
-        lax.psum(square_part.astype(jnp.bfloat16), "smp").astype(jnp.float32),
-    )
-    activated = activate(gate_sum, up_sum, square_sum)
-    ffn_rows = lax.psum_scatter(
-        jnp.dot(activated, w_down, preferred_element_type=jnp.float32).astype(jnp.bfloat16),
-        ("ctx", "head"),
-        scatter_dimension=0,
-        tiled=True,
-    ).astype(jnp.float32)
-    return (own_state.astype(jnp.float32) + ffn_rows).astype(jnp.bfloat16)
+    n, n_smp = lax.axis_size("ctx"), lax.axis_size("smp")
+    pieces = local_out.astype(jnp.bfloat16).reshape(group_rows, n, -1).transpose(1, 0, 2)
+    piece_lse = local_lse.reshape(group_rows, n, -1).transpose(1, 0, 2)
+    state = project(n, n_smp, pieces, piece_lse, w_out[0], residual)
+    return feed_forward(n, n_smp, state, norm_gain[None, :], gate_matrix, w_up, w_down)
 
 
 def solution(mesh):

time: 361 us -> 212 us (0.59)
  waiting for transfers between devices: 217 us -> 0 us
  Pallas kernels: 0 us -> 164 us
  matrix products: 68.3 us -> 15.7 us
  blocking collectives: 13.4 us -> 0 us
  between operations: 13.2 us -> 0.15 us
  starting transfers between devices: 11.6 us -> 0 us
  other arithmetic: 12.6 us -> 4.35 us
    pallas_call x0 -> x2, Pallas kernels: none -> 164 us  [the longest x1 94.6 us: project(): pl.pallas_call(functools.partial(proj_kernel, n, n_smp), out_shape=jax.Sh...]
    reduce_scatter x2 -> x0, waiting for transfers between devices: 84.5 us -> none  [the longest x1 48.2 us: on_device(): lax.psum_scatter(jnp.dot(all_attn, proj_weight, preferred_element_type=jn...]
    psum x1 -> x0, waiting for transfers between devices: 56.8 us -> none  [on_device(): lax.psum(up_part.astype(jnp.bfloat16), 'smp').astype(jnp.float32)]
    all_to_all x2 -> x0, waiting for transfers between devices: 47.6 us -> none  [the longest x1 47.6 us: on_device(): lax.all_to_all(local_out.reshape(group_rows, 1, -1), 'ctx', split_axis=2,...]
    dot_general x4 -> x0, matrix products: 41.6 us -> none  [the longest x1 12.6 us: on_device(): jnp.dot(activated, w_down, preferred_element_type=jnp.float32)]
    all_gather x1 -> x0, waiting for transfers between devices: 27.7 us -> none  [on_device(): state = lax.all_gather(own_state, ('ctx', 'head'), axis=0, tiled=True)]
    all_to_all x2 -> x0, starting transfers between devices: 11.4 us -> none  [the longest x1 6.35 us: on_device(): lax.all_to_all(local_lse.reshape(group_rows, 1, -1), 'ctx', split_axis=2,...]
    all_gather x1 -> x0, blocking collectives: 8.21 us -> none  [on_device(): all_attn = lax.all_gather(attn_slice, 'smp', axis=0, tiled=True)]
  transfers between devices with their start and end apart: 6 -> 0, of which waited for: 5 -> 0; matrix products, arithmetic and copies ran while one was open for 6% -> 0% of each run, Pallas kernels for 0% -> 0%
where the time goes in v1:
time: 212 us
  Pallas kernels  164 us (77%)
  local copies, waits for them, and re-layouts  27.9 us (13%)
  matrix products  15.7 us (7%)
  other arithmetic  4.35 us (2%)
    pallas_call x1, Pallas kernels, project(): pl.pallas_call(functools.partial(proj_kernel, n, n_smp), out_shape=jax.Sh...  94.6 us
    pallas_call x1, Pallas kernels, feed_forward(): pl.pallas_call(functools.partial(ffn_kernel, n, n_smp), out_shape=jax.Sha...  68.9 us
    unnamed x15, local copies, waits for them, and re-layouts  15.3 us
    slice x1, local copies, waits for them, and re-layouts, suffix_piece(): suffix_cache[1].reshape(rows_here, -1, key_value_heads_here, HD)  5.89 us
    dot_general x1, matrix products, suffix_piece(): jnp.einsum('rjgt,rtjd->rjgd', row_weights.astype(jnp.bfloat16), suffix_va...  4.52 us

profile of v1, /device:TPU:0, one launch (start us, length us, event | category | flops | bytes accessed | tf_op | source)
XLA Modules:
  0.0 211.7 jit_solution(3134165868765054840)
XLA Ops:
  0.0 1.8 fusion.38
  1.8 1.3 copy.46
  3.1 0.5 copy.58
  3.7 0.2 copy.62
  3.9 2.5 %multiply_reduce_fusion = (f32[4,128,8]{1,2,0:T(8,128)S(1)}, f32[4,128,8,1024]{3,1,2,0:T(8,128)S(1)}) fusion(bf16[1024,4,128,1]{0,2,3,1:T(8,128)(2,1)S(1)} %bitcast.86, bf16[128,4,8,128]{3,2,1,0:T(8,128)(2,1)S(1)} %bitcast.82), kind=kOutput, calls=%fused_computation.3 | convolution fusion | flops 1082126336 | bytes 18890752 | tf_op jit(solution)/shard_map/sjgd,pjd->jsgp/dot_general | solution.py:547
  6.4 3.7 %fusion.1 = f32[4,128,8]{1,2,0:T(8,128)S(1)} fusion(f32[4,128,8,1024]{3,1,2,0:T(8,128)S(1)} %get-tuple-element.18, f32[4,128,8]{1,2,0:T(8,128)S(1)} %get-tuple-element.17), kind=kLoop, calls=%fused_computation.5 | loop fusion | flops 12578816 | bytes 16809984 | tf_op jit(solution)/shard_map/reduce_sum | solution.py:552
  10.1 4.2 %fusion.9 = bf16[128,4,8,128]{0,3,2,1:T(8,128)(2,1)S(1)} fusion(bf16[1024,4,128,1]{0,2,3,1:T(8,128)(2,1)S(1)} %bitcast.89, f32[4,128,8,1024]{3,1,2,0:T(8,128)S(1)} %get-tuple-element.18, f32[4,128,8]{1,2,0:T(8,128)S(1)} %get-tuple-element.17, f32[128,4,8]{0,2,1:T(8,128)S(1)} %bitcast.91), kind=kOutput, calls=%fused_computation.14 | convolution fusion | flops 1087373312 | bytes 18907136 | tf_op jit(solution)/shard_map/jsgp,pjd->sjgd/dot_general | solution.py:553
  14.3 0.1 compare_select_fusion
  14.4 0.1 convert_reduce_fusion
  14.5 5.9 %fusion.37 = (bf16[1,32,128,1,512]{4,2,3,1,0:T(8,128)(2,1)}, bf16[1,32,128,1,512]{4,2,3,1,0:T(8,128)(2,1)}) fusion(bf16[2,32,128,1,512]{4,2,3,1,0:T(8,128)(2,1)} %param.13), kind=kLoop, calls=%fused_computation.58 | loop fusion | bytes 16777216 | tf_op jit(solution)/shard_map/slice | solution.py:22
  20.4 6.4 %copy.59 = bf16[1,32,128,1,512]{2,4,1,3,0:T(8,128)(2,1)} copy(bf16[1,32,128,1,512]{4,2,3,1,0:T(8,128)(2,1)} %get-tuple-element.14) | data formatting | bytes 8388608
  26.8 0.6 gather_fusion.1
  27.4 0.7 gather_fusion
  28.1 3.5 %fusion.39 = (f32[32,4,8]{2,1,0:T(4,128)S(1)}, f32[32,4,8,128]{3,2,1,0:T(8,128)S(1)}) fusion(bf16[32,128,4,128]{1,3,2,0:T(8,128)(2,1)} %bitcast.80, bf16[32,4,8,128]{3,2,1,0:T(8,128)(2,1)S(1)} %gather_fusion.1, pred[32]{0:T(512)(128)(4,1)S(1)} %get-tuple-element.10, s32[32]{0:T(128)S(1)} %get-tuple-element.9), kind=kOutput, calls=%fused_computation.60 | convolution fusion | flops 34208768 | bytes 4984992 | tf_op jit(solution)/shard_map/rjgd,rtjd->rjgt/dot_general | solution.py:24
  31.8 0.5 fusion.17
  32.3 0.2 add_bitcast_fusion
  32.5 6.4 %copy.60 = bf16[1,32,128,1,512]{2,4,1,3,0:T(8,128)(2,1)} copy(bf16[1,32,128,1,512]{4,2,3,1,0:T(8,128)(2,1)} %get-tuple-element.13) | data formatting | bytes 8388608
  38.9 4.5 %fusion.13 = bf16[32,4,8,128]{3,2,1,0:T(8,128)(2,1)S(1)} fusion(bf16[32,128,4,128]{1,3,2,0:T(8,128)(2,1)} %bitcast.85, f32[32,4,8,128]{3,2,1,0:T(8,128)S(1)} %get-tuple-element.20, f32[32,4,8]{2,1,0:T(4,128)S(1)} %fusion.17, f32[32,4,8]{2,1,0:T(4,128)S(1)} %get-tuple-element.19), kind=kOutput, calls=%fused_computation.18 | convolution fusion | flops 34078720 | bytes 4988928 | tf_op jit(solution)/shard_map/rjgt,rtjd->rjgd/dot_general | solution.py:32
  43.5 0.7 fusion.8
  44.2 1.3 copy.50
  45.6 0.8 copy.51
  46.4 94.6 %shard_map.109.state_ref = bf16[4,2,32,4096]{3,2,1,0:T(8,128)(2,1)} custom-call(bf16[4,128,1024]{2,1,0:T(8,128)(2,1)} %bitcast.84, f32[4,128,8]{2,1,0:T(8,128)} %bitcast.87, bf16[1024,4096]{1,0:T(8,128)(2,1)} %bitcast.81, bf16[32,4096]{1,0:T(8,128)(2,1)} %res_ref.1), custom_call_target="tpu_custom_call" | custom-call | tf_op jit(solution)/shard_map/pallas_call | solution.py:252
  141.0 68.9 %shard_map.110 = bf16[32,4096]{1,0:T(8,128)(2,1)} custom-call(bf16[4,2,32,4096]{3,2,1,0:T(8,128)(2,1)} %shard_map.109.state_ref, f32[1,4096]{1,0:T(1,128)} %bitcast.92, bf16[4096,2048]{1,0:T(8,128)(2,1)} %gate_ref.1, bf16[4096,2048]{1,0:T(8,128)(2,1)} %up_ref.1, bf16[2048,4096]{1,0:T(8,128)(2,1)} %down_ref.1), custom_call_target="tpu_custom_call" | custom-call | tf_op jit(solution)/shard_map/pallas_call | solution.py:486
  210.0 1.7 copy.76
  (15 shorter events, 0.2 us)
Async XLA Ops:
  0.0 27.4 %copy-start = (s32[128]{0:T(128)S(1)}, s32[128]{0:T(128)}, u32[]{:S(2)}) copy-start(s32[128]{0:T(128)} %param.14) | copy-start | bytes 1540
  0.0 3.6 %copy-start.2 = (bf16[128,1,4096]{2,0,1:T(8,128)(2,1)S(1)}, bf16[128,1,4096]{2,0,1:T(8,128)(2,1)}, u32[]{:S(2)}) copy-start(bf16[128,1,4096]{2,0,1:T(8,128)(2,1)} %param.11) | copy-start | bytes 3145732
  6.4 3.7 %copy-start.3 = (bf16[1,1024,1,512]{1,3,2,0:T(8,128)(2,1)S(1)}, bf16[1,1024,1,512]{1,3,2,0:T(8,128)(2,1)}, u32[]{:S(2)}) copy-start(bf16[1,1024,1,512]{1,3,2,0:T(8,128)(2,1)} %copy.46) | copy-start | bytes 3145732
  10.1 4.2 %copy-start.4 = (s32[256]{0:T(256)S(1)}, s32[256]{0:T(256)}, u32[]{:S(2)}) copy-start(s32[256]{0:T(256)} %param.15) | copy-start | bytes 3076
  141.0 70.6 %copy-start.1 = (s32[128]{0:T(128)S(1)}, s32[128]{0:T(128)}, u32[]{:S(2)}) copy-start(s32[128]{0:T(128)} %param.14) | copy-start | bytes 1540

commit v2 on v1

--- a/solution.py
+++ b/solution.py
@@ -16,27 +16,63 @@
 EPSILON = 1e-05
 
 
-def suffix_piece(row_queries, suffix_cache, row_lengths, key_value_heads_here, score_scale):
-    rows_here = suffix_cache.shape[1]
-    suffix_keys = suffix_cache[0].reshape(rows_here, -1, key_value_heads_here, HD)
-    suffix_values = suffix_cache[1].reshape(rows_here, -1, key_value_heads_here, HD)
-    row_scores = (
-        jnp.einsum("rjgd,rtjd->rjgt", row_queries, suffix_keys, preferred_element_type=jnp.float32)
-        * score_scale
+def suffix_kernel(lengths_ref, queries_ref, cache_ref, out_ref, lse_ref):
+    block, heads, _ = queries_ref.shape
+    positions_here, width = cache_ref.shape[2:]
+    per_key = heads // (width // HD)
+    first = pl.program_id(0) * block
+    same = (
+        lax.broadcasted_iota(jnp.int32, (heads, width), 0) // per_key
+        == lax.broadcasted_iota(jnp.int32, (heads, width), 1) // HD
     )
-    positions = lax.broadcasted_iota(jnp.int32, row_scores.shape, 3)
-    row_scores = jnp.where(positions < row_lengths[:, None, None, None], row_scores, -jnp.inf)
-    row_high = jnp.max(row_scores, axis=3)
-    row_weights = jnp.exp(row_scores - row_high[..., None])
-    row_totals = jnp.sum(row_weights, axis=3)
-    row_summed = jnp.einsum(
-        "rjgt,rtjd->rjgd",
-        row_weights.astype(jnp.bfloat16),
-        suffix_values,
-        preferred_element_type=jnp.float32,
-    )
-    row_output = (row_summed / row_totals[..., None]).astype(jnp.bfloat16)
-    return (row_output, row_high + jnp.log(row_totals))
+    positions = lax.broadcasted_iota(jnp.int32, (heads, positions_here), 1)
+    for r in range(block):
+        q = queries_ref[r].astype(jnp.float32)
+        spread = jnp.concatenate([q] * (width // HD), axis=1)
+        spread = jnp.where(same, spread, 0.0).astype(jnp.bfloat16)
+        scores = lax.dot_general(
+            spread, cache_ref[0, r], (((1,), (1,)), ((), ())), preferred_element_type=jnp.float32
+        )
+        scores = jnp.where(positions < lengths_ref[first + r], scores * HD ** (-0.5), -jnp.inf)
+        high = jnp.max(scores, axis=1, keepdims=True)
+        weights = jnp.exp(scores - high)
+        total = jnp.sum(weights, axis=1, keepdims=True)
+        summed = jnp.dot(
+            weights.astype(jnp.bfloat16), cache_ref[1, r], preferred_element_type=jnp.float32
+        )
+        own = jnp.concatenate(
+            [
+                summed[j * per_key : (j + 1) * per_key, j * HD : (j + 1) * HD]
+                for j in range(width // HD)
+            ],
+            axis=0,
+        )
+        out_ref[r] = (own / total).astype(jnp.bfloat16)
+        lse_ref[r] = high + jnp.log(total)
+
+
+def suffix_piece(row_queries, suffix_cache, row_lengths):
+    rows, heads, _ = row_queries.shape
+    block = min(8, rows)
+    _, _, positions_here, width = suffix_cache.shape
+    return pl.pallas_call(
+        suffix_kernel,
+        grid=(rows // block,),
+        out_shape=(
+            jax.ShapeDtypeStruct((rows, heads, HD), jnp.bfloat16),
+            jax.ShapeDtypeStruct((rows, heads, 1), jnp.float32),
+        ),
+        in_specs=[
+            pl.BlockSpec(memory_space=pltpu.SMEM),
+            pl.BlockSpec((block, heads, HD), lambda i: (i, 0, 0)),
+            pl.BlockSpec((2, block, positions_here, width), lambda i: (0, i, 0, 0)),
+        ],
+        out_specs=(
+            pl.BlockSpec((block, heads, HD), lambda i: (i, 0, 0)),
+            pl.BlockSpec((block, heads, 1), lambda i: (i, 0, 0)),
+        ),
+        compiler_params=pltpu.CompilerParams(vmem_limit_bytes=32 * 1024 * 1024),
+    )(row_lengths, row_queries, suffix_cache)
 
 
 MESH = pl.DeviceIdType.MESH
@@ -121,11 +157,15 @@
 def proj_kernel(
     n,
     n_smp,
-    out_ref,
-    lse_ref,
+    q_ref,
+    kv_ref,
+    suf_ref,
+    suf_lse_ref,
     w_ref,
     res_ref,
     state_ref,
+    out_mine,
+    lse_mine,
     out_in,
     lse_in,
     attn,
@@ -152,6 +192,18 @@
 ):
     c, s, h = lax.axis_index("ctx"), lax.axis_index("smp"), lax.axis_index("head")
     tiles = w_buf.shape[0]
+    keys, samples, per_key = suf_lse_ref.shape
+    per_dest = out_mine.shape[2] // HD
+    dests = per_key // per_dest
+    together = 4
+
+    greet(n, n_smp, c, s, h)
+
+    def piece_copies(at, d):
+        return (
+            remote(out_mine.at[d], out_in.at[at], os.at[d], orr.at[at], {"ctx": d}),
+            remote(lse_mine.at[d], lse_in.at[at], ls.at[d], lr.at[at], {"ctx": d}),
+        )
 
     def w_copy(t):
         return pltpu.make_async_copy(w_ref.at[:, columns(t, TILE)], w_buf.at[t], w_sem.at[t])
@@ -160,32 +212,79 @@
     def _(t):
         w_copy(t).start()
 
-    greet(n, n_smp, c, s, h)
-
-    def piece_copies(k):
+    lanes_at = lax.broadcasted_iota(jnp.int32, (samples, 128), 1)
+
+    @pl.loop(0, keys)
+    def _(i):
+        j = lax.rem(lax.div(c, dests) + 1 + i, keys)
+        key = kv_ref[0, :, columns(j, HD)]
+        value = kv_ref[1, :, columns(j, HD)]
+        own = q_ref[:, columns(j, per_key * HD)]
+        placed = suf_ref[:, columns(j, per_key * HD)]
+        placed_lse = suf_lse_ref[j]
+        tables = [jnp.zeros((samples, 128), jnp.float32) for _ in range(dests)]
+        for g0 in range(0, per_key, together):
+            rows = jnp.concatenate(
+                [own[:, g * HD : (g + 1) * HD] for g in range(g0, g0 + together)], axis=0
+            )
+            scores = lax.dot_general(
+                rows, key, (((1,), (1,)), ((), ())), preferred_element_type=jnp.float32
+            ) * HD ** (-0.5)
+            high = jnp.max(scores, axis=1, keepdims=True)
+            weights = jnp.exp(scores - high)
+            total = jnp.sum(weights, axis=1, keepdims=True)
+            summed = (
+                jnp.dot(weights.astype(jnp.bfloat16), value, preferred_element_type=jnp.float32)
+                / total
+            )
+            lse = high + jnp.log(total)
+            for g in range(g0, g0 + together):
+                part = slice((g - g0) * samples, (g - g0 + 1) * samples)
+                own_lse, other_lse = lse[part], placed_lse[:, g : g + 1]
+                top = jnp.maximum(own_lse, other_lse)
+                own_weight = jnp.exp(own_lse - top)
+                other_weight = jnp.exp(other_lse - top)
+                both = own_weight + other_weight
+                merged = (
+                    own_weight * summed[part]
+                    + other_weight * placed[:, g * HD : (g + 1) * HD].astype(jnp.float32)
+                ) / both
+                at = g % per_dest
+                out_mine[j * dests + g // per_dest, :, at * HD : (at + 1) * HD] = merged.astype(
+                    jnp.bfloat16
+                )
+                q = g // per_dest
+                tables[q] = jnp.where(lanes_at == at, top + jnp.log(both), tables[q])
+        for q in range(dests):
+            d = j * dests + q
+            lse_mine[d] = tables[q].T[:8]
+
+            @pl.when(d != c)
+            def _():
+                for copy in piece_copies(c, d):
+                    copy.start()
+
+    for k in range(1, n):
         d = lax.rem(c + k, n)
-        return (
-            remote(out_ref.at[d], out_in.at[k - 1], os.at[k - 1], orr.at[k - 1], {"ctx": d}),
-            remote(lse_ref.at[d], lse_in.at[k - 1], ls.at[k - 1], lr.at[k - 1], {"ctx": d}),
-        )
-
+        for copy in piece_copies(d, d):
+            copy.wait_recv()
     for k in range(1, n):
-        for copy in piece_copies(k):
-            copy.start()
-    for k in range(1, n):
-        for copy in piece_copies(k):
-            copy.wait()
-
-    lses = [lse_ref[c]] + [lse_in[k] for k in range(n - 1)]
+        d = lax.rem(c + k, n)
+        for copy in piece_copies(c, d):
+            copy.wait_send()
+
+    lses = [lse_mine[c]] + [lse_in[lax.rem(c + k, n)] for k in range(1, n)]
     peak = functools.reduce(jnp.maximum, lses)
     scales = [jnp.exp(value - peak) for value in lses]
     denom = functools.reduce(jnp.add, scales)
-    scales = [value / denom for value in scales]
-    for j in range(lse_ref.shape[2]):
+    blank = jnp.zeros((120, samples), jnp.float32)
+    scales = [jnp.concatenate([value / denom, blank], axis=0).T for value in scales]
+    for j in range(per_dest):
         lanes = slice(j * HD, (j + 1) * HD)
-        total = scales[0][:, j : j + 1] * out_ref[c, :, lanes].astype(jnp.float32)
-        for k in range(n - 1):
-            total = total + scales[k + 1][:, j : j + 1] * out_in[k, :, lanes].astype(jnp.float32)
+        total = scales[0][:, j : j + 1] * out_mine[c, :, lanes].astype(jnp.float32)
+        for k in range(1, n):
+            piece = out_in[lax.rem(c + k, n), :, lanes].astype(jnp.float32)
+            total = total + scales[k][:, j : j + 1] * piece
         attn[s, :, lanes] = total.astype(jnp.bfloat16)
 
     def attn_copy(k):
@@ -242,8 +341,9 @@
             pass_copy(t, k).wait()
 
 
-def project(n, n_smp, out, lse, w, residual):
-    count, group_rows, features = out.shape
+def project(n, n_smp, queries, prefix_cache, suffix_out, suffix_lse, w, residual):
+    keys, samples, per_key = suffix_lse.shape
+    features = queries.shape[1] // n
     rows, width = residual.shape
     tiles = width // TILE
     vmem = pl.BlockSpec(memory_space=pltpu.VMEM)
@@ -252,22 +352,24 @@
     return pl.pallas_call(
         functools.partial(proj_kernel, n, n_smp),
         out_shape=jax.ShapeDtypeStruct((n, 2, rows, width), bf16),
-        in_specs=[vmem, vmem, pl.BlockSpec(memory_space=pl.ANY), vmem],
+        in_specs=[vmem, vmem, vmem, vmem, pl.BlockSpec(memory_space=pl.ANY), vmem],
         out_specs=vmem,
         scratch_shapes=[
-            pltpu.VMEM((n - 1, group_rows, features), bf16),
-            pltpu.VMEM((n - 1,) + lse.shape[1:], jnp.float32),
-            pltpu.VMEM((n_smp, group_rows, features), bf16),
+            pltpu.VMEM((n, samples, features), bf16),
+            pltpu.VMEM((n, 8, samples), jnp.float32),
+            pltpu.VMEM((n, samples, features), bf16),
+            pltpu.VMEM((n, 8, samples), jnp.float32),
+            pltpu.VMEM((n_smp, samples, features), bf16),
             pltpu.VMEM((tiles, w.shape[0], TILE), bf16),
             pltpu.VMEM((tiles, 2, n, rows, TILE), bf16),
             pltpu.VMEM((tiles, n, rows, TILE), bf16),
             pltpu.VMEM((tiles, n, rows, TILE), bf16),
             pltpu.VMEM((tiles, n - 1, rows, TILE), bf16),
             dma((tiles,)),
-            dma((n - 1,)),
-            dma((n - 1,)),
-            dma((n - 1,)),
-            dma((n - 1,)),
+            dma((n,)),
+            dma((n,)),
+            dma((n,)),
+            dma((n,)),
             dma((n_smp - 1,)),
             dma((n_smp - 1,)),
             dma((tiles,)),
@@ -282,7 +384,7 @@
         compiler_params=pltpu.CompilerParams(
             collective_id=0, has_side_effects=True, vmem_limit_bytes=VMEM_BYTES
         ),
-    )(out, lse, w, residual)
+    )(queries, prefix_cache, suffix_out, suffix_lse, w, residual)
 
 
 UNITS = 256
@@ -536,65 +638,38 @@
     w_down,
 ):
     group_rows = queries.shape[0]
-    key_value_heads_here = prefix_cache.shape[3] // HD
-    queries_per_key_value = QUERY_HEADS // KEY_VALUE_HEADS
-    heads_local = key_value_heads_here * queries_per_key_value
-    score_scale = HD ** (-0.5)
-    queries_split = queries.reshape(group_rows, key_value_heads_here, queries_per_key_value, HD)
-    prefix_keys = prefix_cache[0].reshape(-1, key_value_heads_here, HD)
-    prefix_values = prefix_cache[1].reshape(-1, key_value_heads_here, HD)
-    scores = (
-        jnp.einsum("sjgd,pjd->jsgp", queries_split, prefix_keys, preferred_element_type=jnp.float32)
-        * score_scale
-    )
-    highest = jnp.max(scores, axis=3)
-    weights = jnp.exp(scores - highest[..., None])
-    totals = jnp.sum(weights, axis=3)
-    summed = jnp.einsum(
-        "jsgp,pjd->sjgd",
-        weights.astype(jnp.bfloat16),
-        prefix_values,
-        preferred_element_type=jnp.float32,
-    )
-    prefix_out = (summed / jnp.transpose(totals, (1, 0, 2))[..., None]).astype(jnp.bfloat16)
-    prefix_lse = jnp.transpose(highest + jnp.log(totals), (1, 0, 2))
+    keys_here = prefix_cache.shape[3] // HD
+    heads_local = queries.shape[2] // HD
+    n, n_smp = lax.axis_size("ctx"), lax.axis_size("smp")
+    own_queries = queries[:, 0]
     rows_here = suffix_cache.shape[1]
-    flat_index = lax.axis_index("ctx") * lax.axis_size("smp") + lax.axis_index("smp")
+    flat_index = lax.axis_index("ctx") * n_smp + lax.axis_index("smp")
     row_ids = lax.dynamic_slice_in_dim(cache_sample, flat_index * rows_here, rows_here, 0)
     local_ids = row_ids % group_rows
-    row_queries = jnp.take(queries_split, local_ids, axis=0)
+    row_queries = jnp.take(own_queries, local_ids, axis=0).reshape(rows_here, heads_local, HD)
     row_lengths = jnp.take(suffix_length, local_ids, axis=0)
-    suffix_out, suffix_lse = suffix_piece(
-        row_queries, suffix_cache, row_lengths, key_value_heads_here, score_scale
+    suffix_out, suffix_lse = suffix_piece(row_queries, suffix_cache[:, :, :, 0], row_lengths)
+    chosen = local_ids[None, :] == jnp.arange(group_rows, dtype=jnp.int32)[:, None]
+    placed_out = jnp.dot(
+        chosen.astype(jnp.bfloat16),
+        suffix_out.reshape(rows_here, -1),
+        preferred_element_type=jnp.float32,
+    ).astype(jnp.bfloat16)
+    placed_lse = jnp.dot(
+        chosen.astype(jnp.float32), suffix_lse[:, :, 0], precision=lax.Precision.HIGHEST
     )
-    onehot = (local_ids[None, :] == jnp.arange(group_rows, dtype=jnp.int32)[:, None]).astype(
-        jnp.float32
+    placed_lse = jnp.where(jnp.any(chosen, axis=1)[:, None], placed_lse, -1e30)
+    placed_lse = placed_lse.reshape(group_rows, keys_here, -1).transpose(1, 0, 2)
+    state = project(
+        n,
+        n_smp,
+        own_queries,
+        prefix_cache[:, :, 0],
+        placed_out,
+        placed_lse,
+        w_out[0],
+        residual,
     )
-    present = jnp.sum(onehot, axis=1)[:, None]
-    placed_out = jnp.dot(
-        onehot,
-        suffix_out.reshape(rows_here, -1).astype(jnp.float32),
-        precision=lax.Precision.HIGHEST,
-    )
-    placed_lse = jnp.dot(
-        onehot, suffix_lse.reshape(rows_here, heads_local), precision=lax.Precision.HIGHEST
-    )
-    own_lse = prefix_lse.reshape(group_rows, heads_local)
-    other_lse = jnp.where(present > 0, placed_lse, own_lse)
-    top = jnp.maximum(own_lse, other_lse)
-    own_weight = jnp.exp(own_lse - top)
-    other_weight = present * jnp.exp(other_lse - top)
-    both_weight = own_weight + other_weight
-    own_values = prefix_out.reshape(group_rows, heads_local, HD).astype(jnp.float32)
-    other_values = placed_out.reshape(group_rows, heads_local, HD)
-    local_out = (
-        own_weight[..., None] * own_values + other_weight[..., None] * other_values
-    ) / both_weight[..., None]
-    local_lse = top + jnp.log(both_weight)
-    n, n_smp = lax.axis_size("ctx"), lax.axis_size("smp")
-    pieces = local_out.astype(jnp.bfloat16).reshape(group_rows, n, -1).transpose(1, 0, 2)
-    piece_lse = local_lse.reshape(group_rows, n, -1).transpose(1, 0, 2)
-    state = project(n, n_smp, pieces, piece_lse, w_out[0], residual)
     return feed_forward(n, n_smp, state, norm_gain[None, :], gate_matrix, w_up, w_down)
 
 

time: 212 us -> 186 us (0.88)
  local copies, waits for them, and re-layouts: 27.9 us -> 8.97 us
  matrix products: 15.7 us -> 1.76 us
  Pallas kernels: 164 us -> 174 us
  other arithmetic: 4.35 us -> 1.19 us
    dot_general x6 -> x2, matrix products: 15.7 us -> 1.76 us  [the longest x1 1.55 us: on_device(): jnp.dot(chosen.astype(jnp.bfloat16), suffix_out.reshape(rows_here, -1), p...]
    pallas_call x0 -> x1, Pallas kernels: none -> 10.6 us  [suffix_piece(): pl.pallas_call(suffix_kernel, grid=(rows // block,), out_shape=(jax.Shape...]
    unnamed x15 -> x8, local copies, waits for them, and re-layouts: 15.3 us -> 5.1 us
    slice x3 -> x0, local copies, waits for them, and re-layouts: 8.98 us -> none  [the longest x1 5.89 us: suffix_piece(): suffix_cache[1].reshape(rows_here, -1, key_value_heads_here, HD)]
    reduce_sum x3 -> x0, other arithmetic: 4.24 us -> none  [the longest x1 3.7 us: on_device(): totals = jnp.sum(weights, axis=3)]
where the time goes in v2:
time: 186 us
  Pallas kernels  174 us (94%)
  local copies, waits for them, and re-layouts  8.97 us (5%)
    pallas_call x1, Pallas kernels, project(): pl.pallas_call(functools.partial(proj_kernel, n, n_smp), out_shape=jax.Sh...  93.9 us
    pallas_call x1, Pallas kernels, feed_forward(): pl.pallas_call(functools.partial(ffn_kernel, n, n_smp), out_shape=jax.Sha...  69.3 us
    pallas_call x1, Pallas kernels, suffix_piece(): pl.pallas_call(suffix_kernel, grid=(rows // block,), out_shape=(jax.Shape...  10.6 us
    unnamed x8, local copies, waits for them, and re-layouts  5.1 us

profile of v2, /device:TPU:0, one launch (start us, length us, event | category | flops | bytes accessed | tf_op | source)
XLA Modules:
  0.0 185.8 jit_solution(16722981638768000717)
XLA Ops:
  0.0 0.0 copy-start
  0.0 0.8 compare_select_fusion
  0.8 0.1 fusion.3
  0.9 0.0 copy-done
  0.9 0.7 gather_fusion
  1.6 2.3 %gather_fusion.1 = bf16[32,4096]{1,0:T(8,128)(2,1)S(1)} fusion(bf16[128,4096]{1,0:T(8,128)(2,1)} %bitcast.18, s32[1024]{0:T(1024)S(1)} %pad_clamp_fusion), kind=kCustom, calls=%fused_computation.1 | custom fusion | bytes 524416 | tf_op jit(solution)/shard_map/jit(_take)/gather | solution.py:649
  4.0 0.1 bitcast_select_fusion.queries_ref
  4.1 0.0 copy-start.2
  4.1 3.4 %copy-done.2 = bf16[2,32,128,1,512]{4,2,3,1,0:T(8,128)(2,1)S(1)} copy-done((bf16[2,32,128,1,512]{4,2,3,1,0:T(8,128)(2,1)S(1)}, bf16[2,32,128,1,512]{4,2,3,1,0:T(8,128)(2,1)}, u32[]{:S(2)}) %copy-start.2) | copy-done | bytes 8388632
  7.5 10.6 %shard_map.109 = (bf16[32,32,128]{2,1,0:T(8,128)(2,1)S(1)}, f32[32,32,1]{2,1,0:T(8,128)S(1)}) custom-call(s32[32]{0:T(128)S(1)} %get-tuple-element.9.lengths_ref, bf16[32,32,128]{2,1,0:T(8,128)(2,1)S(1)} %bitcast_select_fusion.queries_ref, bf16[2,32,128,512]{3,2,1,0:T(8,128)(2,1)S(1)} %bitcast.16), custom_call_target="tpu_custom_call" | custom-call | tf_op jit(solution)/shard_map/pallas_call | solution.py:58
  18.1 0.2 reduce
  18.3 0.2 fusion
  18.5 0.9 copy.13
  19.4 1.5 convolution_convert_fusion.suf_ref
  20.9 93.9 %shard_map.110.state_ref = bf16[4,2,32,4096]{3,2,1,0:T(8,128)(2,1)} custom-call(bf16[128,4096]{1,0:T(8,128)(2,1)} %bitcast.19, bf16[2,1024,512]{2,1,0:T(8,128)(2,1)} %bitcast.21, bf16[128,4096]{1,0:T(8,128)(2,1)} %convolution_convert_fusion.suf_ref, f32[4,128,8]{2,1,0:T(8,128)} %bitcast.23, bf16[1024,4096]{1,0:T(8,128)(2,1)} %bitcast.20, ...), custom_call_target="tpu_custom_call" | custom-call | tf_op jit(solution)/shard_map/pallas_call | solution.py:352
  114.8 0.0 copy-start.1
  114.8 69.3 %shard_map.111 = bf16[32,4096]{1,0:T(8,128)(2,1)} custom-call(bf16[4,2,32,4096]{3,2,1,0:T(8,128)(2,1)} %shard_map.110.state_ref, f32[1,4096]{1,0:T(1,128)} %bitcast.24, bf16[4096,2048]{1,0:T(8,128)(2,1)} %gate_ref.1, bf16[4096,2048]{1,0:T(8,128)(2,1)} %up_ref.1, bf16[2048,4096]{1,0:T(8,128)(2,1)} %down_ref.1), custom_call_target="tpu_custom_call" | custom-call | tf_op jit(solution)/shard_map/pallas_call | solution.py:588
  184.2 1.7 copy.21
  185.8 0.0 copy-done.1
  (3 shorter events, 0.1 us)
Async XLA Ops:
  0.0 0.9 copy-start
  4.1 3.4 %copy-start.2 = (bf16[2,32,128,1,512]{4,2,3,1,0:T(8,128)(2,1)S(1)}, bf16[2,32,128,1,512]{4,2,3,1,0:T(8,128)(2,1)}, u32[]{:S(2)}) copy-start(bf16[2,32,128,1,512]{4,2,3,1,0:T(8,128)(2,1)} %param.13) | copy-start | bytes 25165828
  114.8 71.0 %copy-start.1 = (s32[128]{0:T(128)S(1)}, s32[128]{0:T(128)}, u32[]{:S(2)}) copy-start(s32[128]{0:T(128)} %param.14) | copy-start | bytes 1540

commit v3 on v2

--- a/solution.py
+++ b/solution.py
@@ -103,11 +103,23 @@
     pl.semaphore_wait(barrier, (n - 1) + (n_smp - 1) + 1)
 
 
-class Scatter:
-    def __init__(self, n, c, h, buf_a, recv_a, buf_b, recv_b, sa, ra, sb, rb):
+class Line:
+    def __init__(self, n, c, h, buf_a, recv_a, buf_b, from_left, from_right, sa, ra, ss, rl, rr):
         self.n, self.c, self.h = n, c, h
-        self.buf_a, self.recv_a, self.buf_b, self.recv_b = buf_a, recv_a, buf_b, recv_b
-        self.sa, self.ra, self.sb, self.rb = sa, ra, sb, rb
+        self.buf_a, self.recv_a, self.buf_b = buf_a, recv_a, buf_b
+        self.from_left, self.from_right = from_left, from_right
+        self.sa, self.ra, self.ss, self.rl, self.rr = sa, ra, ss, rl, rr
+        self.tiles = buf_a.shape[0]
+
+        @pl.when(c == 0)
+        def _():
+            from_left[:, 0] = jnp.zeros(from_left.shape[:1] + from_left.shape[2:], from_left.dtype)
+
+        @pl.when(c == n - 1)
+        def _():
+            from_right[:, n - 1] = jnp.zeros(
+                from_right.shape[:1] + from_right.shape[2:], from_right.dtype
+            )
 
     def pair_copy(self, t):
         return remote(
@@ -118,14 +130,22 @@
             {"head": 1 - self.h},
         )
 
-    def row_copy(self, t, k):
-        d = lax.rem(self.c + k, self.n)
+    def to_right(self, t, d):
         return remote(
             self.buf_b.at[t, d],
-            self.recv_b.at[t, k - 1],
-            self.sb.at[t, k - 1],
-            self.rb.at[t, k - 1],
-            {"ctx": d},
+            self.from_left.at[t, d],
+            self.ss.at[t, d],
+            self.rl.at[t, d],
+            {"ctx": lax.rem(self.c + 1, self.n)},
+        )
+
+    def to_left(self, t, d):
+        return remote(
+            self.buf_b.at[t, d],
+            self.from_right.at[t, d],
+            self.ss.at[t, d],
+            self.rr.at[t, d],
+            {"ctx": lax.rem(self.c + self.n - 1, self.n)},
         )
 
     def give(self, t, value):
@@ -139,15 +159,57 @@
         self.pair_copy(t).wait()
         both = self.buf_a[t, self.h].astype(jnp.float32) + self.recv_a[t].astype(jnp.float32)
         self.buf_b[t] = both.astype(jnp.bfloat16)
-        for k in range(1, self.n):
-            self.row_copy(t, k).start()
+
+    def hop(self, t, inside, d, copy_of, arrived, first):
+        @pl.when(inside & (t >= 0) & (t < self.tiles))
+        def _():
+            @pl.when(jnp.logical_not(first))
+            def _():
+                copy_of(t, d).wait_recv()
+                both = self.buf_b[t, d].astype(jnp.float32) + arrived[t, d].astype(jnp.float32)
+                self.buf_b[t, d] = both.astype(jnp.bfloat16)
+
+            copy_of(t, d).start()
+
+    def step(self, i):
+        n, c = self.n, self.c
+
+        @pl.when((i >= 1) & (i <= self.tiles))
+        def _():
+            self.middle(i - 1)
+
+        for e in range(n - 1):
+            right, left = n - 1 - e, e
+            self.hop(i - 1 - c, right > c, right, self.to_right, self.from_left, c == 0)
+            self.hop(i - n + c, left < c, left, self.to_left, self.from_right, c == n - 1)
 
     def finish(self, t):
-        total = self.buf_b[t, self.c].astype(jnp.float32)
-        for k in range(1, self.n):
-            self.row_copy(t, k).wait()
-            total = total + self.recv_b[t, k - 1].astype(jnp.float32)
-        return total
+        n, c = self.n, self.c
+
+        @pl.when(c > 0)
+        def _():
+            self.to_right(t, c).wait_recv()
+
+        @pl.when(c < n - 1)
+        def _():
+            self.to_left(t, c).wait_recv()
+
+        return (
+            self.buf_b[t, c].astype(jnp.float32)
+            + self.from_left[t, c].astype(jnp.float32)
+            + self.from_right[t, c].astype(jnp.float32)
+        )
+
+    def drain(self, t):
+        for d in range(self.n):
+
+            @pl.when(d > self.c)
+            def _():
+                self.to_right(t, d).wait_send()
+
+            @pl.when(d < self.c)
+            def _():
+                self.to_left(t, d).wait_send()
 
 
 def columns(t, width):
@@ -173,7 +235,8 @@
     buf_a,
     recv_a,
     buf_b,
-    recv_b,
+    from_left,
+    from_right,
     w_sem,
     os,
     orr,
@@ -183,9 +246,11 @@
     xr,
     sa,
     ra,
-    sb,
-    rb,
-    gs,
+    ss,
+    rl,
+    rr,
+    gsr,
+    gsl,
     gr,
     fs,
     fr,
@@ -297,48 +362,68 @@
     for k in range(1, n_smp):
         attn_copy(k).wait()
 
-    scatter = Scatter(n, c, h, buf_a, recv_a, buf_b, recv_b, sa, ra, sb, rb)
+    line = Line(n, c, h, buf_a, recv_a, buf_b, from_left, from_right, sa, ra, ss, rl, rr)
+
+    def gather_copy(t, q, way, sems):
+        block = state_ref.at[q, h, :, columns(t, TILE)]
+        return remote(
+            block, block, sems.at[t, q], gr.at[t, q], {"ctx": lax.rem(c + way, n)}
+        )
+
+    def pass_copy(t, q):
+        block = state_ref.at[q, h, :, columns(t, TILE)]
+        return remote(block, block, fs.at[t, q], fr.at[t, q], {"head": 1 - h})
+
+    def spread(t, q, right, left):
+        @pl.when(right & (c < n - 1))
+        def _():
+            gather_copy(t, q, 1, gsr).start()
+
+        @pl.when(left & (c > 0))
+        def _():
+            gather_copy(t, q, n - 1, gsl).start()
+
+        pass_copy(t, q).start()
+
+    @pl.loop(0, tiles + 2 * n - 1)
+    def _(i):
+        @pl.when(i < tiles)
+        def _():
+            w_copy(i).wait()
+            rows = attn[...].reshape(-1, attn.shape[2])
+            line.give(i, jnp.dot(rows, w_buf[i], preferred_element_type=jnp.float32))
+
+        line.step(i)
+
+        @pl.when((i >= n) & (i < tiles + n))
+        def _():
+            t = i - n
+            own = line.finish(t) + res_ref[:, columns(t, TILE)].astype(jnp.float32)
+            state_ref[c, h, :, columns(t, TILE)] = own.astype(jnp.bfloat16)
+            spread(t, c, c >= 0, c >= 0)
+
+        for q in range(n):
+            t = i - n - lax.max(c - q, q - c)
+
+            @pl.when((q != c) & (t >= 0) & (t < tiles))
+            def _():
+                gather_copy(t, q, 1, gsr).wait_recv()
+                spread(t, q, q < c, q > c)
 
     @pl.loop(0, tiles)
     def _(t):
-        w_copy(t).wait()
-        rows = attn[...].reshape(-1, attn.shape[2])
-        scatter.give(t, jnp.dot(rows, w_buf[t], preferred_element_type=jnp.float32))
-
-        @pl.when(t >= 1)
-        def _():
-            scatter.middle(t - 1)
-
-    scatter.middle(tiles - 1)
-
-    def gather_copy(t, k):
-        block = state_ref.at[c, h, :, columns(t, TILE)]
-        return remote(
-            block, block, gs.at[t, k - 1], gr.at[t, k - 1], {"ctx": lax.rem(c + k, n)}
-        )
-
-    def pass_copy(t, k):
-        block = state_ref.at[lax.rem(c + n - k, n), h, :, columns(t, TILE)]
-        return remote(block, block, fs.at[t, k], fr.at[t, k], {"head": 1 - h})
-
-    @pl.loop(0, tiles)
-    def _(t):
-        own = scatter.finish(t) + res_ref[:, columns(t, TILE)].astype(jnp.float32)
-        state_ref[c, h, :, columns(t, TILE)] = own.astype(jnp.bfloat16)
-        for k in range(1, n):
-            gather_copy(t, k).start()
-        pass_copy(t, 0).start()
-
-    @pl.loop(0, tiles)
-    def _(t):
-        for k in range(1, n):
-            gather_copy(t, k).wait()
-            pass_copy(t, k).start()
-
-    @pl.loop(0, tiles)
-    def _(t):
-        for k in range(n):
-            pass_copy(t, k).wait()
+        line.drain(t)
+        for q in range(n):
+
+            @pl.when((q <= c) & (c < n - 1))
+            def _():
+                gather_copy(t, q, 1, gsr).wait_send()
+
+            @pl.when((q >= c) & (c > 0))
+            def _():
+                gather_copy(t, q, n - 1, gsl).wait_send()
+
+            pass_copy(t, q).wait()
 
 
 def project(n, n_smp, queries, prefix_cache, suffix_out, suffix_lse, w, residual):
@@ -364,7 +449,8 @@
             pltpu.VMEM((tiles, 2, n, rows, TILE), bf16),
             pltpu.VMEM((tiles, n, rows, TILE), bf16),
             pltpu.VMEM((tiles, n, rows, TILE), bf16),
-            pltpu.VMEM((tiles, n - 1, rows, TILE), bf16),
+            pltpu.VMEM((tiles, n, rows, TILE), bf16),
+            pltpu.VMEM((tiles, n, rows, TILE), bf16),
             dma((tiles,)),
             dma((n,)),
             dma((n,)),
@@ -374,10 +460,12 @@
             dma((n_smp - 1,)),
             dma((tiles,)),
             dma((tiles,)),
-            dma((tiles, n - 1)),
-            dma((tiles, n - 1)),
-            dma((tiles, n - 1)),
-            dma((tiles, n - 1)),
+            dma((tiles, n)),
+            dma((tiles, n)),
+            dma((tiles, n)),
+            dma((tiles, n)),
+            dma((tiles, n)),
+            dma((tiles, n)),
             dma((tiles, n)),
             dma((tiles, n)),
         ],
@@ -412,7 +500,8 @@
     buf_a,
     recv_a,
     buf_b,
-    recv_b,
+    from_left,
+    from_right,
     g_sem,
     u_sem,
     d_sem,
@@ -424,8 +513,9 @@
     hr,
     sa,
     ra,
-    sb,
-    rb,
+    ss,
+    rl,
+    rr,
 ):
     c, s, h = lax.axis_index("ctx"), lax.axis_index("smp"), lax.axis_index("head")
     steps = part.shape[0]
@@ -555,23 +645,26 @@
         for k in range(1, n_smp):
             hidden_copy(t, k).wait()
 
-    scatter = Scatter(n, c, h, buf_a, recv_a, buf_b, recv_b, sa, ra, sb, rb)
+    line = Line(n, c, h, buf_a, recv_a, buf_b, from_left, from_right, sa, ra, ss, rl, rr)
+
+    @pl.loop(0, tiles + n)
+    def _(i):
+        @pl.when(i < tiles)
+        def _():
+            down_copy(i).wait()
+            line.give(i, jnp.dot(hidden[...], down_buf[i], preferred_element_type=jnp.float32))
+
+        line.step(i)
+
+        @pl.when(i >= n)
+        def _():
+            t = i - n
+            own = line.finish(t) + state_ref[c, h, :, columns(t, TILE)].astype(jnp.float32)
+            mixed_ref[:, columns(t, TILE)] = own.astype(jnp.bfloat16)
 
     @pl.loop(0, tiles)
     def _(t):
-        down_copy(t).wait()
-        scatter.give(t, jnp.dot(hidden[...], down_buf[t], preferred_element_type=jnp.float32))
-
-        @pl.when(t >= 1)
-        def _():
-            scatter.middle(t - 1)
-
-    scatter.middle(tiles - 1)
-
-    @pl.loop(0, tiles)
-    def _(t):
-        own = scatter.finish(t) + state_ref[c, h, :, columns(t, TILE)].astype(jnp.float32)
-        mixed_ref[:, columns(t, TILE)] = own.astype(jnp.bfloat16)
+        line.drain(t)
 
 
 def feed_forward(n, n_smp, state, gain, gate, up, down):
@@ -603,7 +696,8 @@
             pltpu.VMEM((tiles, 2, n, rows, TILE), bf16),
             pltpu.VMEM((tiles, n, rows, TILE), bf16),
             pltpu.VMEM((tiles, n, rows, TILE), bf16),
-            pltpu.VMEM((tiles, n - 1, rows, TILE), bf16),
+            pltpu.VMEM((tiles, n, rows, TILE), bf16),
+            pltpu.VMEM((tiles, n, rows, TILE), bf16),
             dma((slots,)),
             dma((slots,)),
             dma((tiles,)),
@@ -615,8 +709,9 @@
             dma((steps, n_smp - 1)),
             dma((tiles,)),
             dma((tiles,)),
-            dma((tiles, n - 1)),
-            dma((tiles, n - 1)),
+            dma((tiles, n)),
+            dma((tiles, n)),
+            dma((tiles, n)),
         ],
         compiler_params=pltpu.CompilerParams(
             collective_id=1, has_side_effects=True, vmem_limit_bytes=VMEM_BYTES

time: 186 us -> 180 us (0.968)
  Pallas kernels: 174 us -> 168 us
    pallas_call x1, Pallas kernels: 93.9 us -> 85.5 us  [project(): pl.pallas_call(functools.partial(proj_kernel, n, n_smp), out_shape=jax.Sh...]
    pallas_call x1, Pallas kernels: 69.3 us -> 72.1 us  [feed_forward(): pl.pallas_call(functools.partial(ffn_kernel, n, n_smp), out_shape=jax.Sha...]
where the time goes in v3:
time: 180 us
  Pallas kernels  168 us (93%)
  local copies, waits for them, and re-layouts  8.97 us (5%)
    pallas_call x1, Pallas kernels, project(): pl.pallas_call(functools.partial(proj_kernel, n, n_smp), out_shape=jax.Sh...  85.5 us
    pallas_call x1, Pallas kernels, feed_forward(): pl.pallas_call(functools.partial(ffn_kernel, n, n_smp), out_shape=jax.Sha...  72.1 us
    pallas_call x1, Pallas kernels, suffix_piece(): pl.pallas_call(suffix_kernel, grid=(rows // block,), out_shape=(jax.Shape...  10.6 us
    unnamed x8, local copies, waits for them, and re-layouts  5.1 us

profile of v3, /device:TPU:0, one launch (start us, length us, event | category | flops | bytes accessed | tf_op | source)
XLA Modules:
  0.0 180.2 jit_solution(7553279007778430402)
XLA Ops:
  0.0 0.0 copy-start
  0.0 0.8 compare_select_fusion
  0.8 0.1 fusion.3
  0.9 0.0 copy-done
  0.9 0.7 gather_fusion
  1.6 2.3 %gather_fusion.1 = bf16[32,4096]{1,0:T(8,128)(2,1)S(1)} fusion(bf16[128,4096]{1,0:T(8,128)(2,1)} %bitcast.18, s32[1024]{0:T(1024)S(1)} %pad_clamp_fusion), kind=kCustom, calls=%fused_computation.1 | custom fusion | bytes 524416 | tf_op jit(solution)/shard_map/jit(_take)/gather | solution.py:744
  4.0 0.1 bitcast_select_fusion.queries_ref
  4.1 0.0 copy-start.2
  4.1 3.4 %copy-done.2 = bf16[2,32,128,1,512]{4,2,3,1,0:T(8,128)(2,1)S(1)} copy-done((bf16[2,32,128,1,512]{4,2,3,1,0:T(8,128)(2,1)S(1)}, bf16[2,32,128,1,512]{4,2,3,1,0:T(8,128)(2,1)}, u32[]{:S(2)}) %copy-start.2) | copy-done | bytes 8388632
  7.5 10.6 %shard_map.109 = (bf16[32,32,128]{2,1,0:T(8,128)(2,1)S(1)}, f32[32,32,1]{2,1,0:T(8,128)S(1)}) custom-call(s32[32]{0:T(128)S(1)} %get-tuple-element.9.lengths_ref, bf16[32,32,128]{2,1,0:T(8,128)(2,1)S(1)} %bitcast_select_fusion.queries_ref, bf16[2,32,128,512]{3,2,1,0:T(8,128)(2,1)S(1)} %bitcast.16), custom_call_target="tpu_custom_call" | custom-call | tf_op jit(solution)/shard_map/pallas_call | solution.py:58
  18.1 0.2 reduce
  18.3 0.2 fusion
  18.5 0.9 copy.13
  19.4 1.5 convolution_convert_fusion.suf_ref
  20.9 85.5 %shard_map.110.state_ref = bf16[4,2,32,4096]{3,2,1,0:T(8,128)(2,1)} custom-call(bf16[128,4096]{1,0:T(8,128)(2,1)} %bitcast.19, bf16[2,1024,512]{2,1,0:T(8,128)(2,1)} %bitcast.21, bf16[128,4096]{1,0:T(8,128)(2,1)} %convolution_convert_fusion.suf_ref, f32[4,128,8]{2,1,0:T(8,128)} %bitcast.23, bf16[1024,4096]{1,0:T(8,128)(2,1)} %bitcast.20, ...), custom_call_target="tpu_custom_call" | custom-call | tf_op jit(solution)/shard_map/pallas_call | solution.py:437
  106.4 0.0 copy-start.1
  106.4 72.1 %shard_map.111 = bf16[32,4096]{1,0:T(8,128)(2,1)} custom-call(bf16[4,2,32,4096]{3,2,1,0:T(8,128)(2,1)} %shard_map.110.state_ref, f32[1,4096]{1,0:T(1,128)} %bitcast.24, bf16[4096,2048]{1,0:T(8,128)(2,1)} %gate_ref.1, bf16[4096,2048]{1,0:T(8,128)(2,1)} %up_ref.1, bf16[2048,4096]{1,0:T(8,128)(2,1)} %down_ref.1), custom_call_target="tpu_custom_call" | custom-call | tf_op jit(solution)/shard_map/pallas_call | solution.py:681
  178.5 1.7 copy.21
  180.2 0.0 copy-done.1
  (3 shorter events, 0.1 us)
Async XLA Ops:
  0.0 0.9 copy-start
  4.1 3.4 %copy-start.2 = (bf16[2,32,128,1,512]{4,2,3,1,0:T(8,128)(2,1)S(1)}, bf16[2,32,128,1,512]{4,2,3,1,0:T(8,128)(2,1)}, u32[]{:S(2)}) copy-start(bf16[2,32,128,1,512]{4,2,3,1,0:T(8,128)(2,1)} %param.13) | copy-start | bytes 25165828
  106.4 73.8 %copy-start.1 = (s32[128]{0:T(128)S(1)}, s32[128]{0:T(128)}, u32[]{:S(2)}) copy-start(s32[128]{0:T(128)} %param.14) | copy-start | bytes 1540

commit v4 on v2

--- a/solution.py
+++ b/solution.py
@@ -71,12 +71,13 @@
             pl.BlockSpec((block, heads, HD), lambda i: (i, 0, 0)),
             pl.BlockSpec((block, heads, 1), lambda i: (i, 0, 0)),
         ),
-        compiler_params=pltpu.CompilerParams(vmem_limit_bytes=32 * 1024 * 1024),
+        compiler_params=pltpu.CompilerParams(vmem_limit_bytes=VMEM_BYTES),
     )(row_lengths, row_queries, suffix_cache)
 
 
 MESH = pl.DeviceIdType.MESH
 TILE = 512
+LAG = 3
 VMEM_BYTES = 62 * 1024 * 1024
 
 
@@ -185,7 +186,8 @@
     ra,
     sb,
     rb,
-    gs,
+    gsr,
+    gsl,
     gr,
     fs,
     fr,
@@ -299,46 +301,67 @@
 
     scatter = Scatter(n, c, h, buf_a, recv_a, buf_b, recv_b, sa, ra, sb, rb)
 
+    def gather_copy(t, q, way, sems):
+        block = state_ref.at[q, h, :, columns(t, TILE)]
+        return remote(
+            block, block, sems.at[t, q], gr.at[t, q], {"ctx": lax.rem(c + way, n)}
+        )
+
+    def pass_copy(t, q):
+        block = state_ref.at[q, h, :, columns(t, TILE)]
+        return remote(block, block, fs.at[t, q], fr.at[t, q], {"head": 1 - h})
+
+    def spread(t, q, right, left):
+        @pl.when(right & (c < n - 1))
+        def _():
+            gather_copy(t, q, 1, gsr).start()
+
+        @pl.when(left & (c > 0))
+        def _():
+            gather_copy(t, q, n - 1, gsl).start()
+
+        pass_copy(t, q).start()
+
+    @pl.loop(0, tiles + LAG + n - 1)
+    def _(i):
+        @pl.when(i < tiles)
+        def _():
+            w_copy(i).wait()
+            rows = attn[...].reshape(-1, attn.shape[2])
+            scatter.give(i, jnp.dot(rows, w_buf[i], preferred_element_type=jnp.float32))
+
+        @pl.when((i >= 1) & (i <= tiles))
+        def _():
+            scatter.middle(i - 1)
+
+        @pl.when((i >= LAG) & (i < tiles + LAG))
+        def _():
+            t = i - LAG
+            own = scatter.finish(t) + res_ref[:, columns(t, TILE)].astype(jnp.float32)
+            state_ref[c, h, :, columns(t, TILE)] = own.astype(jnp.bfloat16)
+            spread(t, c, c >= 0, c >= 0)
+
+        for q in range(n):
+            t = i - LAG - lax.max(c - q, q - c)
+
+            @pl.when((q != c) & (t >= 0) & (t < tiles))
+            def _():
+                gather_copy(t, q, 1, gsr).wait_recv()
+                spread(t, q, q < c, q > c)
+
     @pl.loop(0, tiles)
     def _(t):
-        w_copy(t).wait()
-        rows = attn[...].reshape(-1, attn.shape[2])
-        scatter.give(t, jnp.dot(rows, w_buf[t], preferred_element_type=jnp.float32))
-
-        @pl.when(t >= 1)
-        def _():
-            scatter.middle(t - 1)
-
-    scatter.middle(tiles - 1)
-
-    def gather_copy(t, k):
-        block = state_ref.at[c, h, :, columns(t, TILE)]
-        return remote(
-            block, block, gs.at[t, k - 1], gr.at[t, k - 1], {"ctx": lax.rem(c + k, n)}
-        )
-
-    def pass_copy(t, k):
-        block = state_ref.at[lax.rem(c + n - k, n), h, :, columns(t, TILE)]
-        return remote(block, block, fs.at[t, k], fr.at[t, k], {"head": 1 - h})
-
-    @pl.loop(0, tiles)
-    def _(t):
-        own = scatter.finish(t) + res_ref[:, columns(t, TILE)].astype(jnp.float32)
-        state_ref[c, h, :, columns(t, TILE)] = own.astype(jnp.bfloat16)
-        for k in range(1, n):
-            gather_copy(t, k).start()
-        pass_copy(t, 0).start()
-
-    @pl.loop(0, tiles)
-    def _(t):
-        for k in range(1, n):
-            gather_copy(t, k).wait()
-            pass_copy(t, k).start()
-
-    @pl.loop(0, tiles)
-    def _(t):
-        for k in range(n):
-            pass_copy(t, k).wait()
+        for q in range(n):
+
+            @pl.when((q <= c) & (c < n - 1))
+            def _():
+                gather_copy(t, q, 1, gsr).wait_send()
+
+            @pl.when((q >= c) & (c > 0))
+            def _():
+                gather_copy(t, q, n - 1, gsl).wait_send()
+
+            pass_copy(t, q).wait()
 
 
 def project(n, n_smp, queries, prefix_cache, suffix_out, suffix_lse, w, residual):
@@ -376,8 +399,9 @@
             dma((tiles,)),
             dma((tiles, n - 1)),
             dma((tiles, n - 1)),
-            dma((tiles, n - 1)),
-            dma((tiles, n - 1)),
+            dma((tiles, n)),
+            dma((tiles, n)),
+            dma((tiles, n)),
             dma((tiles, n)),
             dma((tiles, n)),
         ],
@@ -646,10 +670,13 @@
     flat_index = lax.axis_index("ctx") * n_smp + lax.axis_index("smp")
     row_ids = lax.dynamic_slice_in_dim(cache_sample, flat_index * rows_here, rows_here, 0)
     local_ids = row_ids % group_rows
-    row_queries = jnp.take(own_queries, local_ids, axis=0).reshape(rows_here, heads_local, HD)
-    row_lengths = jnp.take(suffix_length, local_ids, axis=0)
+    chosen = local_ids[None, :] == jnp.arange(group_rows, dtype=jnp.int32)[:, None]
+    row_queries = jnp.dot(
+        chosen.T.astype(jnp.bfloat16), own_queries, preferred_element_type=jnp.float32
+    ).astype(jnp.bfloat16)
+    row_queries = row_queries.reshape(rows_here, heads_local, HD)
+    row_lengths = jnp.sum(jnp.where(chosen, suffix_length[:, None], 0), axis=0)
     suffix_out, suffix_lse = suffix_piece(row_queries, suffix_cache[:, :, :, 0], row_lengths)
-    chosen = local_ids[None, :] == jnp.arange(group_rows, dtype=jnp.int32)[:, None]
     placed_out = jnp.dot(
         chosen.astype(jnp.bfloat16),
         suffix_out.reshape(rows_here, -1),

time: 186 us -> 182 us (0.978)
  local copies, waits for them, and re-layouts: 8.97 us -> 3.27 us
  Pallas kernels: 174 us -> 170 us
  matrix products: 1.76 us -> 4.22 us
  other arithmetic: 1.19 us -> 3.51 us
    pallas_call x1, Pallas kernels: 93.9 us -> 89 us  [project(): pl.pallas_call(functools.partial(proj_kernel, n, n_smp), out_shape=jax.Sh...]
    gather x2 -> x0, local copies, waits for them, and re-layouts: 3.02 us -> none  [the longest x1 2.32 us: on_device(): jnp.take(own_queries, local_ids, axis=0).reshape(rows_here, heads_local, HD)]
    unnamed x8 -> x2, local copies, waits for them, and re-layouts: 5.1 us -> 2.42 us
where the time goes in v4:
time: 182 us; the launch traced here: 181 us
  Pallas kernels  170 us (93%)
  matrix products  4.22 us (2%)
  other arithmetic  3.51 us (2%)
  local copies, waits for them, and re-layouts  3.27 us (2%)
    pallas_call x1, Pallas kernels, project(): pl.pallas_call(functools.partial(proj_kernel, n, n_smp), out_shape=jax.Sh...  89 us
    pallas_call x1, Pallas kernels, feed_forward(): pl.pallas_call(functools.partial(ffn_kernel, n, n_smp), out_shape=jax.Sha...  69.3 us
    pallas_call x1, Pallas kernels, suffix_piece(): pl.pallas_call(suffix_kernel, grid=(rows // block,), out_shape=(jax.Shape...  12 us

profile of v4, /device:TPU:0, one launch (start us, length us, event | category | flops | bytes accessed | tf_op | source)
XLA Modules:
  0.0 181.3 jit_solution(9914169092847335297)
XLA Ops:
  0.0 0.8 and_select_fusion
  0.8 1.4 select_reduce_fusion.lengths_ref
  2.2 0.1 fusion.4
  2.3 1.5 fusion
  3.8 0.7 copy.14
  4.5 12.0 %shard_map.109 = (bf16[32,32,128]{2,1,0:T(8,128)(2,1)}, f32[32,32,1]{2,1,0:T(8,128)}) custom-call(s32[32]{0:T(128)} %select_reduce_fusion.lengths_ref, bf16[32,32,128]{2,1,0:T(8,128)(2,1)} %bitcast.22, bf16[2,32,128,512]{3,2,1,0:T(8,128)(2,1)} %bitcast.18), custom_call_target="tpu_custom_call" | custom-call | tf_op jit(solution)/shard_map/pallas_call | solution.py:58
  16.5 1.2 reduce
  17.8 0.2 fusion.1
  18.0 0.9 copy.13
  18.8 2.5 %convolution_convert_fusion.suf_ref = bf16[128,4096]{1,0:T(8,128)(2,1)} fusion(bf16[4,8,32,128]{3,2,1,0:T(8,128)(2,1)} %bitcast.24, s32[32]{0:T(128)S(1)} %and_select_fusion), kind=kOutput, calls=%fused_computation | convolution fusion | flops 34082816 | bytes 1310848 | tf_op jit(solution)/shard_map/dot_general | solution.py:680
  21.3 89.0 %shard_map.110.state_ref = bf16[4,2,32,4096]{3,2,1,0:T(8,128)(2,1)} custom-call(bf16[128,4096]{1,0:T(8,128)(2,1)} %bitcast.20, bf16[2,1024,512]{2,1,0:T(8,128)(2,1)} %bitcast.21, bf16[128,4096]{1,0:T(8,128)(2,1)} %convolution_convert_fusion.suf_ref, f32[4,128,8]{2,1,0:T(8,128)} %bitcast.23, bf16[1024,4096]{1,0:T(8,128)(2,1)} %bitcast.19, ...), custom_call_target="tpu_custom_call" | custom-call | tf_op jit(solution)/shard_map/pallas_call | solution.py:375
  110.3 69.3 %shard_map.111 = bf16[32,4096]{1,0:T(8,128)(2,1)} custom-call(bf16[4,2,32,4096]{3,2,1,0:T(8,128)(2,1)} %shard_map.110.state_ref, f32[1,4096]{1,0:T(1,128)} %bitcast.25, bf16[4096,2048]{1,0:T(8,128)(2,1)} %gate_ref.1, bf16[4096,2048]{1,0:T(8,128)(2,1)} %up_ref.1, bf16[2048,4096]{1,0:T(8,128)(2,1)} %down_ref.1), custom_call_target="tpu_custom_call" | custom-call | tf_op jit(solution)/shard_map/pallas_call | solution.py:612
  179.6 1.7 copy.21

commit v5 on v3

--- a/solution.py
+++ b/solution.py
@@ -71,7 +71,7 @@
             pl.BlockSpec((block, heads, HD), lambda i: (i, 0, 0)),
             pl.BlockSpec((block, heads, 1), lambda i: (i, 0, 0)),
         ),
-        compiler_params=pltpu.CompilerParams(vmem_limit_bytes=32 * 1024 * 1024),
+        compiler_params=pltpu.CompilerParams(vmem_limit_bytes=57 * 1024 * 1024),
     )(row_lengths, row_queries, suffix_cache)
 
 
@@ -210,6 +210,53 @@
             @pl.when(d < self.c)
             def _():
                 self.to_left(t, d).wait_send()
+
+
+class Scatter:
+    def __init__(self, n, c, h, buf_a, recv_a, buf_b, recv_b, sa, ra, sb, rb):
+        self.n, self.c, self.h = n, c, h
+        self.buf_a, self.recv_a, self.buf_b, self.recv_b = buf_a, recv_a, buf_b, recv_b
+        self.sa, self.ra, self.sb, self.rb = sa, ra, sb, rb
+
+    def pair_copy(self, t):
+        return remote(
+            self.buf_a.at[t, 1 - self.h],
+            self.recv_a.at[t],
+            self.sa.at[t],
+            self.ra.at[t],
+            {"head": 1 - self.h},
+        )
+
+    def row_copy(self, t, k):
+        d = lax.rem(self.c + k, self.n)
+        return remote(
+            self.buf_b.at[t, d],
+            self.recv_b.at[t, k - 1],
+            self.sb.at[t, k - 1],
+            self.rb.at[t, k - 1],
+            {"ctx": d},
+        )
+
+    def give(self, t, value):
+        _, _, n, rows, width = self.buf_a.shape
+        parts = value.reshape(n, 2, rows, width).astype(jnp.bfloat16)
+        self.buf_a[t, 0] = parts[:, 0]
+        self.buf_a[t, 1] = parts[:, 1]
+        self.pair_copy(t).start()
+
+    def middle(self, t):
+        self.pair_copy(t).wait()
+        both = self.buf_a[t, self.h].astype(jnp.float32) + self.recv_a[t].astype(jnp.float32)
+        self.buf_b[t] = both.astype(jnp.bfloat16)
+        for k in range(1, self.n):
+            self.row_copy(t, k).start()
+
+    def finish(self, t):
+        total = self.buf_b[t, self.c].astype(jnp.float32)
+        for k in range(1, self.n):
+            self.row_copy(t, k).wait()
+            total = total + self.recv_b[t, k - 1].astype(jnp.float32)
+        return total
 
 
 def columns(t, width):
@@ -500,8 +547,7 @@
     buf_a,
     recv_a,
     buf_b,
-    from_left,
-    from_right,
+    recv_b,
     g_sem,
     u_sem,
     d_sem,
@@ -513,9 +559,8 @@
     hr,
     sa,
     ra,
-    ss,
-    rl,
-    rr,
+    sb,
+    rb,
 ):
     c, s, h = lax.axis_index("ctx"), lax.axis_index("smp"), lax.axis_index("head")
     steps = part.shape[0]
@@ -645,26 +690,23 @@
         for k in range(1, n_smp):
             hidden_copy(t, k).wait()
 
-    line = Line(n, c, h, buf_a, recv_a, buf_b, from_left, from_right, sa, ra, ss, rl, rr)
-
-    @pl.loop(0, tiles + n)
-    def _(i):
-        @pl.when(i < tiles)
-        def _():
-            down_copy(i).wait()
-            line.give(i, jnp.dot(hidden[...], down_buf[i], preferred_element_type=jnp.float32))
-
-        line.step(i)
-
-        @pl.when(i >= n)
-        def _():
-            t = i - n
-            own = line.finish(t) + state_ref[c, h, :, columns(t, TILE)].astype(jnp.float32)
-            mixed_ref[:, columns(t, TILE)] = own.astype(jnp.bfloat16)
+    scatter = Scatter(n, c, h, buf_a, recv_a, buf_b, recv_b, sa, ra, sb, rb)
 
     @pl.loop(0, tiles)
     def _(t):
-        line.drain(t)
+        down_copy(t).wait()
+        scatter.give(t, jnp.dot(hidden[...], down_buf[t], preferred_element_type=jnp.float32))
+
+        @pl.when(t >= 1)
+        def _():
+            scatter.middle(t - 1)
+
+    scatter.middle(tiles - 1)
+
+    @pl.loop(0, tiles)
+    def _(t):
+        own = scatter.finish(t) + state_ref[c, h, :, columns(t, TILE)].astype(jnp.float32)
+        mixed_ref[:, columns(t, TILE)] = own.astype(jnp.bfloat16)
 
 
 def feed_forward(n, n_smp, state, gain, gate, up, down):
@@ -696,8 +738,7 @@
             pltpu.VMEM((tiles, 2, n, rows, TILE), bf16),
             pltpu.VMEM((tiles, n, rows, TILE), bf16),
             pltpu.VMEM((tiles, n, rows, TILE), bf16),
-            pltpu.VMEM((tiles, n, rows, TILE), bf16),
-            pltpu.VMEM((tiles, n, rows, TILE), bf16),
+            pltpu.VMEM((tiles, n - 1, rows, TILE), bf16),
             dma((slots,)),
             dma((slots,)),
             dma((tiles,)),
@@ -709,9 +750,8 @@
             dma((steps, n_smp - 1)),
             dma((tiles,)),
             dma((tiles,)),
-            dma((tiles, n)),
-            dma((tiles, n)),
-            dma((tiles, n)),
+            dma((tiles, n - 1)),
+            dma((tiles, n - 1)),
         ],
         compiler_params=pltpu.CompilerParams(
             collective_id=1, has_side_effects=True, vmem_limit_bytes=VMEM_BYTES

time: 180 us -> 179 us (level)
  local copies, waits for them, and re-layouts: 8.97 us -> 5.59 us
  other arithmetic: 1.19 us -> 3.52 us
  Pallas kernels: 168 us -> 166 us
    unnamed x8 -> x6, local copies, waits for them, and re-layouts: 5.1 us -> 1.72 us
    pallas_call x1, Pallas kernels: 72.1 us -> 68.9 us  [feed_forward(): pl.pallas_call(functools.partial(ffn_kernel, n, n_smp), out_shape=jax.Sha...]
where the time goes in v5:
time: 179 us; the launch traced here: 178 us
  Pallas kernels  166 us (93%)
  local copies, waits for them, and re-layouts  5.59 us (3%)
  other arithmetic  3.52 us (2%)
  matrix products  2.69 us (2%)
    pallas_call x1, Pallas kernels, project(): pl.pallas_call(functools.partial(proj_kernel, n, n_smp), out_shape=jax.Sh...  85.5 us
    pallas_call x1, Pallas kernels, feed_forward(): pl.pallas_call(functools.partial(ffn_kernel, n, n_smp), out_shape=jax.Sha...  68.9 us
    pallas_call x1, Pallas kernels, suffix_piece(): pl.pallas_call(suffix_kernel, grid=(rows // block,), out_shape=(jax.Shape...  12 us

profile of v5, /device:TPU:0, one launch (start us, length us, event | category | flops | bytes accessed | tf_op | source)
XLA Modules:
  0.0 178.2 jit_solution(13672538014682459026)
XLA Ops:
  0.0 0.0 copy-start
  0.0 0.8 compare_select_fusion
  0.8 0.1 fusion.3
  0.9 0.0 copy-done
  0.9 0.7 gather_fusion
  1.6 0.6 broadcast_select_fusion
  2.2 2.3 %gather_fusion.1 = bf16[32,4096]{1,0:T(8,128)(2,1)S(1)} fusion(bf16[128,4096]{1,0:T(8,128)(2,1)} %bitcast.16, s32[1024]{0:T(1024)S(1)} %pad_clamp_fusion), kind=kCustom, calls=%fused_computation.1 | custom fusion | bytes 524416 | tf_op jit(solution)/shard_map/jit(_take)/gather | solution.py:784
  4.5 0.8 bitcast_select_fusion.queries_ref
  5.3 12.0 %shard_map.109 = (bf16[32,32,128]{2,1,0:T(8,128)(2,1)}, f32[32,32,1]{2,1,0:T(8,128)}) custom-call(s32[32]{0:T(128)} %get-tuple-element.9.lengths_ref, bf16[32,32,128]{2,1,0:T(8,128)(2,1)} %bitcast_select_fusion.queries_ref, bf16[2,32,128,512]{3,2,1,0:T(8,128)(2,1)} %bitcast.18), custom_call_target="tpu_custom_call" | custom-call | tf_op jit(solution)/shard_map/pallas_call | solution.py:58
  17.3 1.2 reduce
  18.6 0.2 fusion
  18.8 0.9 copy.13
  19.6 2.5 %convolution_convert_fusion.suf_ref = bf16[128,4096]{1,0:T(8,128)(2,1)} fusion(bf16[4,8,32,128]{3,2,1,0:T(8,128)(2,1)} %bitcast.23, s32[32]{0:T(128)S(1)} %get-tuple-element.12), kind=kOutput, calls=%fused_computation.2 | convolution fusion | flops 34082816 | bytes 1310848 | tf_op jit(solution)/shard_map/dot_general | solution.py:788
  22.1 85.5 %shard_map.110.state_ref = bf16[4,2,32,4096]{3,2,1,0:T(8,128)(2,1)} custom-call(bf16[128,4096]{1,0:T(8,128)(2,1)} %bitcast.17, bf16[2,1024,512]{2,1,0:T(8,128)(2,1)} %bitcast.20, bf16[128,4096]{1,0:T(8,128)(2,1)} %convolution_convert_fusion.suf_ref, f32[4,128,8]{2,1,0:T(8,128)} %bitcast.22, bf16[1024,4096]{1,0:T(8,128)(2,1)} %bitcast.19, ...), custom_call_target="tpu_custom_call" | custom-call | tf_op jit(solution)/shard_map/pallas_call | solution.py:484
  107.6 0.0 copy-start.1
  107.6 68.9 %shard_map.111 = bf16[32,4096]{1,0:T(8,128)(2,1)} custom-call(bf16[4,2,32,4096]{3,2,1,0:T(8,128)(2,1)} %shard_map.110.state_ref, f32[1,4096]{1,0:T(1,128)} %bitcast.24, bf16[4096,2048]{1,0:T(8,128)(2,1)} %gate_ref.1, bf16[4096,2048]{1,0:T(8,128)(2,1)} %up_ref.1, bf16[2048,4096]{1,0:T(8,128)(2,1)} %down_ref.1), custom_call_target="tpu_custom_call" | custom-call | tf_op jit(solution)/shard_map/pallas_call | solution.py:723
  176.5 1.7 copy.21
  178.2 0.0 copy-done.1
  (2 shorter events, 0.0 us)
Async XLA Ops:
  0.0 0.9 copy-start
  107.6 70.6 %copy-start.1 = (s32[128]{0:T(128)S(1)}, s32[128]{0:T(128)}, u32[]{:S(2)}) copy-start(s32[128]{0:T(128)} %param.14) | copy-start | bytes 1540
